TPU v7x, 32 devices: a whole 2x2x4 slice. The times are simulated.
32 devices in a mesh: dp: 8 (over z, y), tensor: 4 (over x, core).
Axes of the slice: x: 2, y: 2, z: 4, core: 2. Of those that a mesh axis runs over, the one named last changes fastest.
Arguments:
- tokens: bfloat16 [32, 1024, 768], P('dp', 'tensor'), may hold values from -6 to 6
- segments: int32 [32, 1024], P('dp'), may hold values from 0 to 17, as said below
- qkv_weight: bfloat16 [3, 768, 768], P(None, 'dp', 'tensor'), may hold values from -0.3125 to 0.3125
- out_weight: bfloat16 [768, 768], P('tensor', 'dp'), may hold values from -0.625 to 0.625
- in_weight: bfloat16 [768, 3072], P('dp', 'tensor'), may hold values from -0.21875 to 0.21875
- down_weight: bfloat16 [3072, 768], P('tensor', 'dp'), may hold values from -0.15625 to 0.15625
- vectors: float32 [12, 768], P(None, ('dp', 'tensor')), may hold values from -0.9 to 1.75
- cotangent: bfloat16 [32, 1024, 768], P('dp', 'tensor'), may hold values from -6 to 6
Outputs:
- output: bfloat16 [32, 1024, 768], P('dp', 'tensor')
- grad_tokens: bfloat16 [32, 1024, 768], P('dp', 'tensor')
- query_key_value_gradient: float32 [3, 768, 768], P(None, 'dp', 'tensor')
- out_weight_gradient: float32 [768, 768], P('tensor', 'dp')
- in_weight_gradient: float32 [768, 3072], P('dp', 'tensor')
- down_weight_gradient: float32 [3072, 768], P('tensor', 'dp')
- grad_vectors: float32 [12, 768], P(None, ('dp', 'tensor'))
Inputs may be any that keep to these rules, and one draw needn't show every extreme that they name: `segments`: within each sequence the numbers start at 0 and rise by one where a document begins; documents have 60 to 800 tokens, except the last of a sequence, which the sequence's end may cut.
All inputs are finite; a program needn't handle non-finite values.
Results may differ from a plain program's by a relative error of at most 0.022.
Values may be sent and summed in bfloat16 or wider, within the bound.
A program may use at most 256 MiB of HBM per device.

v0:
```python
import functools

import jax
import jax.numpy as jnp
from jax import lax
from jax.experimental import pallas as pl
from jax.experimental.pallas import tpu as pltpu
from jax.sharding import PartitionSpec as P

HD = 64
LANES = 128
EPS = 1e-05
MASKED = -1e30
SEGS = 32
TOP = 35
LOG2E = 1.4426950408889634
QSCALE = LOG2E * HD**-0.5
BF = jnp.bfloat16
F32 = jnp.float32
ALL = ("dp", "tensor")
MESH = pl.DeviceIdType.MESH
ANY = pl.BlockSpec(memory_space=pl.ANY)
VMEM = pl.BlockSpec(memory_space=pltpu.VMEM)
NT = (((1,), (1,)), ((), ()))
NN = (((1,), (0,)), ((), ()))
TN = (((0,), (0,)), ((), ()))
SLOTS = ((0, (0, 1)), (1, (2,)))


def mm(a, b, dims=NN):
    return lax.dot_general(a, b, dims, preferred_element_type=F32)


def lane_ids(shape):
    return lax.broadcasted_iota(jnp.int32, shape, 1)


def low_half(shape):
    return lane_ids(shape) < HD


def swap_halves(value):
    return pltpu.roll(value, HD, 1)


def tile(ref, t, i, rows=slice(None)):
    return ref[t, rows, i * LANES : (i + 1) * LANES]


def flat(value):
    return value.reshape(-1, value.shape[-1])


def at_tick(step, ticks):
    for when, work in ticks:
        pl.when(step == when)(functools.partial(work))


def group_biases(vt):
    length = vt.shape[0]
    groups = length // (3 * HD)
    lanes = lane_ids((length, LANES))
    q, v = vt[:, 6:7], vt[:, 7:8]
    zero = jnp.zeros((LANES, 1), F32)
    out = jnp.zeros((length, LANES), F32)
    for t in range(groups):
        a, b, c = 3 * HD * t, 3 * HD * t + LANES, 3 * HD * (t + 1)
        column = jnp.concatenate([q[a:b], zero, v[a:b], q[b:c], zero[:HD], zero, v[b:c], zero[:HD]], axis=0)
        out = jnp.where(lanes == t, column, out)
    return out.T


def fwd_setup(vt_v, seg, vec_rows, bias_v, oh_v, km_v):
    vt = flat(vt_v[...])
    vec_rows[...] = vt.T[: vec_rows.shape[0]]
    biases = group_biases(vt)
    for t in range(bias_v.shape[0]):
        bias_v[t] = biases[t : t + 1]
    place = lane_ids(oh_v.shape) % HD
    same = seg[...] == place
    oh_v[...] = jnp.where(same, 1.0, 0.0).astype(BF)
    km_v[...] = key_marks(seg, km_v.shape)


def key_marks(seg, shape):
    place = lane_ids(shape) % HD
    marks = jnp.where(place < SEGS, jnp.where(seg[...] == place, 0.0, MASKED), 1.0)
    return jnp.where(place < TOP, marks, 0.0).astype(BF)


def fwd_group(t, x_v, a_v, bias_v, km_v, qkv_v, ka_v, va_v):
    x = flat(x_v[...])
    w = flat(a_v[...])
    low = low_half((x.shape[0], LANES))
    for i in range(6):
        cols = slice(i * LANES, (i + 1) * LANES)
        out = mm(x, w[:, cols]) + bias_v[t, :, cols]
        if i % 3 == 0:
            out = out * QSCALE
        out = out.astype(BF)
        qkv_v[t, :, cols] = out
        one = jnp.ones_like(out)
        if i == 1:
            ka_v[0] = jnp.where(low, out, km_v[...])
            ka_v[1] = jnp.where(low, km_v[...], out)
        if i == 2:
            va_v[0] = jnp.where(low, out, one)
            va_v[1] = jnp.where(low, one, out)
        if i == 4:
            ka_v[2] = jnp.where(low, out, km_v[...])
        if i == 5:
            va_v[2] = jnp.where(low, out, one)


def fwd_block(t, rows, block, qkv_v, ka_v, va_v, oh_v, ctx_v, lse_ref):
    shape = (block, LANES)
    low = low_half(shape)
    lanes = lane_ids(shape)
    marks = oh_v[rows, :]
    lse = lse_ref[rows, :]
    parts = []
    for h in range(3):
        q = tile(qkv_v, t, 0 if h < 2 else 3, rows)
        q = jnp.where(low, marks, q) if h == 1 else jnp.where(low, q, marks)
        s = mm(q, ka_v[h], NT)
        top = jnp.max(s, axis=1, keepdims=True)
        w = jnp.exp2(s - top).astype(BF)
        o = mm(w, va_v[h])
        total = o[:, HD : HD + 1] if h != 1 else o[:, 0:1]
        lse = jnp.where(lanes == 3 * t + h, top + jnp.log2(total), lse)
        parts.append(o)
    lse_ref[rows, :] = lse
    sums = swap_halves(jnp.where(low, parts[1], parts[0]))
    pair = jnp.where(low, parts[0], parts[1]) / sums
    last = parts[2] / swap_halves(parts[2])
    zero = jnp.zeros(shape, F32)
    tiles = (pair, swap_halves(pair), swap_halves(last))
    for i, value in enumerate(tiles):
        ctx_v[t, rows, i * LANES : (i + 1) * LANES] = jnp.where(low, zero, value).astype(BF)


def spread(base, value, lanes):
    hi = value.astype(BF).astype(F32)
    rest = value - hi
    mid = rest.astype(BF).astype(F32)
    low = rest - mid
    place = lanes % HD
    out = jnp.where(place == SEGS, hi, jnp.where(place == SEGS + 1, mid, jnp.where(place == SEGS + 2, low, 0.0)))
    return jnp.where(place < SEGS, base, out.astype(BF))


def bwd_group(t, qkv, ctx, dctx, lse, oh_v, km_v, qa_v, ka_v, va_v, da_v, kt_v, dqt_v):
    length = oh_v.shape[0]
    shape = (length, LANES)
    low = low_half(shape)
    lanes = lane_ids(shape)
    oh, km = oh_v[...], km_v[...]
    ones = jnp.where((lanes % HD >= SEGS) & (lanes % HD < TOP), 1.0, 0.0).astype(BF)

    def cols(ref, i):
        return ref[:, i * LANES : (i + 1) * LANES]

    q, k, v = cols(qkv, 0), cols(qkv, 1), cols(qkv, 2)
    q2, k2, v2 = cols(qkv, 3), cols(qkv, 4), cols(qkv, 5)
    c_pair = jnp.where(low, swap_halves(cols(ctx, 1)), cols(ctx, 0))
    d_pair = jnp.where(low, swap_halves(cols(dctx, 1)), cols(dctx, 0))
    c_last = swap_halves(cols(ctx, 2))
    d_last = swap_halves(cols(dctx, 2))
    prod = c_pair.astype(F32) * d_pair.astype(F32)
    prod2 = c_last.astype(F32) * d_last.astype(F32)
    lse_all = lse[...]
    zero = jnp.zeros_like(prod)
    for h in range(3):
        mine = low if h != 1 else jnp.logical_not(low)
        delta = jnp.sum(jnp.where(mine, prod2 if h == 2 else prod, zero), axis=1, keepdims=True)
        top = jnp.sum(jnp.where(lanes == 3 * t + h, lse_all, zero), axis=1, keepdims=True)
        qa_v[h] = jnp.where(mine, q2 if h == 2 else q, spread(oh, -top, lanes))
        da_v[h] = jnp.where(mine, d_last if h == 2 else d_pair, spread(jnp.zeros_like(oh), -delta, lanes))
        ka_v[h] = jnp.where(mine, k2 if h == 2 else k, km)
        va_v[h] = jnp.where(mine, v2 if h == 2 else v, ones)
    kt_v[0] = k.T
    kt_v[1] = k2.T
    dqt_v[...] = jnp.zeros_like(dqt_v)


def bwd_block(rows, block, qa_v, ka_v, va_v, da_v, kt_v, dqt_v, out):
    low = low_half((block, LANES))
    dk, dv = [], []
    for h in range(3):
        s = mm(ka_v[h, rows, :], qa_v[h], NT)
        p = jnp.exp2(s)
        dv.append(mm(p.astype(BF), da_v[h]))
        dp = mm(va_v[h, rows, :], da_v[h], NT)
        ds = (p * dp).astype(BF)
        dk.append(mm(ds, qa_v[h]) * (1.0 / LOG2E))
        slot, half = h // 2, slice((h % 2) * HD, (h % 2 + 1) * HD)
        dqt_v[slot, half, :] += mm(kt_v[slot, half, rows], ds)
    zero = jnp.zeros((block, LANES), F32)
    tiles = {
        1: jnp.where(low, dk[0], dk[1]),
        2: jnp.where(low, dv[0], dv[1]),
        4: jnp.where(low, dk[2], zero),
        5: jnp.where(low, dv[2], zero),
    }
    for i, value in tiles.items():
        out[rows, i * LANES : (i + 1) * LANES] = value.astype(BF)


def bwd_finish(dqt_v, out):
    scale = HD**-0.5
    low = low_half((out.shape[0], LANES))
    out[:, 0:LANES] = (dqt_v[0].T * scale).astype(BF)
    last = dqt_v[1].T * scale
    out[:, 3 * LANES : 4 * LANES] = jnp.where(low, last, jnp.zeros_like(last)).astype(BF)


def normalize(values, gain_row, shift_row):
    average = jnp.mean(values, axis=-1, keepdims=True)
    centered = values - average
    variance = jnp.mean(centered * centered, axis=-1, keepdims=True)
    inverse = lax.rsqrt(variance + EPS)
    unit = centered * inverse
    return unit * gain_row + shift_row, unit, inverse


def normalize_back(upstream, unit, inverse, gain_row):
    d_unit = upstream * gain_row
    first = jnp.mean(d_unit, axis=-1, keepdims=True)
    second = jnp.mean(d_unit * unit, axis=-1, keepdims=True)
    return inverse * (d_unit - first - unit * second)


def eighths(value):
    return jnp.sum(value.reshape(-1, 8, value.shape[-1]), axis=0)


def gelu_both(x):
    a = jnp.abs(x)
    tail = jnp.exp2(x * x * (-0.5 * LOG2E))
    t = 1.0 / (1.0 + (0.3275911 * 0.5**0.5) * a)
    poly = ((((1.061405429 * t - 1.453152027) * t + 1.421413741) * t - 0.284496736) * t + 0.254829592) * t
    rest = 0.5 * poly * tail
    cdf = jnp.where(x < 0, rest, 1.0 - rest)
    return x * cdf, cdf + x * tail * 0.3989422804014327


def mid_rows(i, block, refs):
    (x_v, cot_v, ctx_v, ao_v, in_v, dn_v, vec, act_v, dact_v, dpre_v, y1_v, g2_v, out_v, gh1_v, dctx_v, sums_v) = refs
    rows = pl.ds(pl.multiple_of(i * block, block), block)
    groups = in_v.shape[0]

    def row(k):
        return vec[k : k + 1, :]

    def note(k, value):
        sums_v[k] += eighths(value)

    attn = mm(ctx_v[0, rows, :], ao_v[0], NT)
    for t in range(1, groups):
        attn = attn + mm(ctx_v[t, rows, :], ao_v[t], NT)
    h1 = x_v[i].astype(F32) + attn + row(4)
    y1, u1, r1 = normalize(h1, row(0), row(1))
    y1_low = y1.astype(BF)
    y1_v[rows, :] = y1_low
    ffn = row(5) + y1
    for t in range(groups):
        pre = mm(y1_low, in_v[t]) + row(8 + t)
        act, slope = gelu_both(pre)
        act = act.astype(BF)
        act_v[t, rows, :] = act
        dact_v[t] = slope.astype(BF)
        ffn = ffn + mm(act, dn_v[t], NT)
    out, u2, r2 = normalize(ffn, row(2), row(3))
    out_v[i] = out.astype(BF)
    up = cot_v[i].astype(F32)
    g_h2 = normalize_back(up, u2, r2, row(2))
    note(2, up * u2)
    note(3, up)
    note(5, g_h2)
    g2 = g_h2.astype(BF)
    g2_v[rows, :] = g2
    g_y1 = g_h2
    for t in range(groups):
        dpre = (mm(g2, dn_v[t]) * dact_v[t].astype(F32)).astype(BF)
        dpre_v[t, rows, :] = dpre
        note(8 + t, dpre.astype(F32))
        g_y1 = g_y1 + mm(dpre, in_v[t], NT)
    note(0, g_y1 * u1)
    note(1, g_y1)
    g_h1 = normalize_back(g_y1, u1, r1, row(0))
    note(4, g_h1)
    gh1_v[i] = g_h1
    g1 = g_h1.astype(BF)
    for t in range(groups):
        dctx_v[t, rows, :] = mm(g1, ao_v[t]).astype(BF)

STEP = {"z2": 4, "z1": 2, "y": 1, "x": 2, "c": 1}
BLOCKS = ("x", "c", "z2", "z1", "y")
FEATURES = ("z2", "z1", "y", "x", "c")
P_Y = ("z2", "z1", "x", "y")
P_Z = ("z2", "x", "y", "z1")
P_X = ("z2", "y", "z1", "x")


class Place:
    def __init__(self):
        self.d = lax.axis_index("dp")
        self.t = lax.axis_index("tensor")
        self.bit = {
            "x": self.t // 2,
            "c": self.t % 2,
            "z2": self.d // 4,
            "z1": (self.d // 2) % 2,
            "y": self.d % 2,
        }

    def flip(self, dim):
        return 1 - self.bit[dim]

    def peer(self, dim):
        move = STEP[dim] * (1 - 2 * self.bit[dim])
        if dim in ("x", "c"):
            return (self.d, self.t + move)
        return (self.d + move, self.t)

    def row_peer(self, k):
        t = self.t
        if k in (1, 3):
            t = t + (1 - 2 * self.bit["c"])
        if k in (2, 3):
            t = t + 2 * (1 - 2 * self.bit["x"])
        return t

    def index(self, dims, **chosen):
        return tuple(chosen.get(dim, self.bit[dim]) for dim in dims)


def enter(place):
    bar = pltpu.get_barrier_semaphore()
    peers = [place.peer(dim) for dim in BLOCKS] + [(place.d, place.row_peer(3))]
    for peer in peers:
        pl.semaphore_signal(bar, inc=1, device_id=peer, device_id_type=MESH)
    pl.semaphore_wait(bar, len(peers))


class Copies:
    def __init__(self, send, recv, local):
        self.send, self.recv, self.local = send, recv, local
        self.count = self.locals = 0

    def remote(self, ends):
        i = self.count
        self.count += 1

        def copy():
            src, dst, peer = ends()
            return pltpu.make_async_remote_copy(
                src_ref=src,
                dst_ref=dst,
                send_sem=self.send.at[i],
                recv_sem=self.recv.at[i],
                device_id=peer,
                device_id_type=MESH,
            )

        copy().start()
        return lambda: copy().wait()

    def here(self, ends):
        i = self.locals
        self.locals += 1

        def copy():
            src, dst = ends()
            return pltpu.make_async_copy(src, dst, self.local.at[i])

        copy().start()
        return lambda: copy().wait()


ALLBITS = slice(None)


class GatherPart:
    def __init__(self, place, copies, own, full, order, rows, dims=BLOCKS):
        self.place, self.copies, self.own, self.full, self.order = place, copies, own, full, order
        self.rows, self.dims = rows, dims
        self.stage = 0
        self.side = []

    def at(self, **chosen):
        return self.full.at[self.place.index(self.dims, **chosen) + (self.rows,)]

    def begin(self):
        p, c = self.place, self.copies
        self.current = c.remote(lambda: (self.own.at[self.rows], self.at(), p.peer(self.order[0])))
        self.side.append(c.remote(lambda: (self.own.at[self.rows], self.at(), p.peer("c"))))
        self.keep = c.here(lambda: (self.own.at[self.rows], self.at()))

    def held(self, s):
        return self.at(**{dim: ALLBITS for dim in self.order[:s]})

    def arrived(self, s):
        dim = self.order[s]
        return self.at(**{other: ALLBITS for other in self.order[:s]}, **{dim: self.place.flip(dim)})

    def advance(self):
        p, c, s = self.place, self.copies, self.stage
        self.current()
        if s == 0:
            self.keep()
        if s + 1 < len(self.order):
            self.current = c.remote(lambda: (self.held(s + 1), self.held(s + 1), p.peer(self.order[s + 1])))
        self.side.append(c.remote(lambda: (self.arrived(s), self.arrived(s), p.peer("c"))))
        self.stage = s + 1

    def finish(self):
        wait_all(self.side)


def every(count, work):
    if count == 0:
        work(())
        return

    def body(i, carry):
        work(tuple((i // 2**j) % 2 for j in reversed(range(count))))
        return carry

    lax.fori_loop(0, 2**count, body, 0)


def blockwise(ref):
    return ref.reshape(2 ** (len(ref.shape) - 2), *ref.shape[-2:])


def spot(bits):
    place = 0
    for bit in bits:
        place = 2 * place + bit
    return place


class ReducePart:
    def __init__(self, place, copies, src, total, arrive, out, order, rows, dims=BLOCKS):
        self.place, self.copies, self.src, self.total, self.arrive = place, copies, src, total, arrive
        self.out, self.order, self.rows, self.dims = out, order, rows, dims
        self.inner = tuple(dim for dim in dims if dim != "c")
        self.kept = self.inner
        if total is None:
            self.total, self.kept = src, dims
        self.stage = 0

    def source(self, **chosen):
        return self.src.at[self.place.index(self.dims, **chosen) + (self.rows,)]

    def sums(self, **chosen):
        return self.total.at[self.place.index(self.kept, **chosen) + (self.rows,)]

    def half(self, bit):
        p, first = self.place, self.order[0]

        def ends():
            free = {dim: ALLBITS for dim in self.inner}
            free[first] = bit()
            dst = self.arrive[0].at[p.index(self.inner, **free) + (self.rows,)]
            return self.source(c=p.flip("c"), **free), dst, p.peer("c")

        return self.copies.remote(ends)

    def begin(self):
        p, first = self.place, self.order[0]
        self.side = [self.half(lambda: p.flip(first)), self.half(lambda: p.bit[first])]
        if self.kept is self.inner:
            free = {dim: ALLBITS for dim in self.inner}
            self.keep = self.copies.here(lambda: (self.source(**free), self.sums(**free)))

    def add(self, fixed, bit):
        s = self.stage
        left = [dim for dim in self.inner if dim not in self.order[:s]] if s else list(self.inner)
        loose = [dim for dim in left if dim != fixed]

        total, arrive = blockwise(self.total), blockwise(self.arrive[s])

        def work(bits):
            chosen = dict(zip(loose, bits))
            chosen[fixed] = bit
            mine = spot(self.place.index(self.kept, **chosen))
            there = spot(tuple(chosen[dim] for dim in left))
            both = total[mine, self.rows, :].astype(F32) + arrive[there, self.rows, :].astype(F32)
            total[mine, self.rows, :] = both.astype(total.dtype)

        every(len(loose), work)

    def send(self):
        p, s = self.place, self.stage
        dim = self.order[s]
        free = {other: ALLBITS for other in self.order[s + 1 :]}

        def ends():
            src = self.sums(**free, **{dim: p.flip(dim)})
            dst = self.arrive[s + 1].at[(ALLBITS,) * len(free) + (self.rows,)]
            return src, dst, p.peer(dim)

        return self.copies.remote(ends)

    def advance(self):
        p, s = self.place, self.stage
        if s == 0:
            if self.kept is self.inner:
                self.keep()
            self.side[0]()
        else:
            self.current()
        if s < len(self.order):
            dim = self.order[s]
            self.add(dim, p.flip(dim))
            self.current = self.send()
            if s == 0:
                self.side[1]()
            self.add(dim, p.bit[dim])
        else:
            mine = spot(self.place.index(self.kept))
            self.out[self.rows, :] = blockwise(self.total)[mine, self.rows, :].astype(F32) + self.arrive[s][self.rows, :].astype(F32)
        self.stage = s + 1


def arrivals(rows, cols, dtype):
    return [pltpu.VMEM((2,) * n + (rows, cols), dtype) for n in (4, 3, 2, 1, 0)]


def start_row(place, copies, src, dst, k):
    def ends():
        to = place.row_peer(k)
        return src.at[to], dst.at[place.t], (place.d, to)

    return copies.remote(ends)


def keep_row(place, copies, src, dst):
    return copies.here(lambda: (src.at[place.t], dst.at[place.t]))


def start_rows(place, copies, src, dst):
    return [start_row(place, copies, src, dst, k) for k in (2, 3, 1)] + [keep_row(place, copies, src, dst)]


def wait_all(waits):
    for wait in waits:
        wait()


def params(collective=None):
    more = {} if collective is None else {"collective_id": collective, "has_side_effects": True}
    return pltpu.CompilerParams(vmem_limit_bytes=60 << 20, **more)


def sems(count):
    return [pltpu.SemaphoreType.DMA((count,))] * 2


def fwd_core(group_ref, x_v, vt_v, seg, qkv, ctx, lse, vec_rows, s, ticks):
    (a_v, bias_v, oh_v, km_v, qkv_v, ka_v, va_v, ctx_v, a_sem, out_sem) = s
    groups, length = qkv.shape[:2]
    block = 256
    blocks = length // block

    def load(t):
        return pltpu.make_async_copy(group_ref(t), a_v.at[t % 2], a_sem.at[t % 2])

    load(0).start()
    fwd_setup(vt_v, seg, vec_rows, bias_v, oh_v, km_v)
    lse[...] = jnp.zeros_like(lse)

    def step(i, carry):
        t, b = i // blocks, i % blocks
        at_tick(i, ticks)

        @pl.when(b == 0)
        def _():
            load(t).wait()

            @pl.when(t + 1 < groups)
            def _():
                load(t + 1).start()

            fwd_group(t, x_v, a_v.at[t % 2], bias_v, km_v, qkv_v, ka_v, va_v)
            pltpu.make_async_copy(qkv_v.at[t], qkv.at[t], out_sem.at[0, t]).start()

        rows = pl.ds(pl.multiple_of(b * block, block), block)
        fwd_block(t, rows, block, qkv_v, ka_v, va_v, oh_v, ctx_v, lse)

        @pl.when(b == blocks - 1)
        def _():
            pltpu.make_async_copy(ctx_v.at[t], ctx.at[t], out_sem.at[1, t]).start()

        return carry

    lax.fori_loop(0, groups * blocks, step, 0)
    for t in range(groups):
        pltpu.make_async_copy(qkv_v.at[t], qkv.at[t], out_sem.at[0, t]).wait()
        pltpu.make_async_copy(ctx_v.at[t], ctx.at[t], out_sem.at[1, t]).wait()


def fwd_scratch(groups, length, width):
    return [
        pltpu.VMEM((2, 2, 2, 2, width // 8, width), BF),
        pltpu.VMEM((groups, 1, width), F32),
        pltpu.VMEM((length, LANES), BF),
        pltpu.VMEM((length, LANES), BF),
        pltpu.VMEM((groups, length, width), BF),
        pltpu.VMEM((3, length, LANES), BF),
        pltpu.VMEM((3, length, LANES), BF),
        pltpu.VMEM((groups, length, 3 * LANES), BF),
        pltpu.SemaphoreType.DMA((2,)),
        pltpu.SemaphoreType.DMA((2, groups)),
    ]


def fwd_shapes(groups, length, width):
    return [
        jax.ShapeDtypeStruct((groups, length, width), BF),
        jax.ShapeDtypeStruct((groups, length, 3 * LANES), BF),
        jax.ShapeDtypeStruct((length, LANES), F32),
        jax.ShapeDtypeStruct((16, width), F32),
    ]


def fwd_comm_kernel(shard, vec, tok, cot, seg, g, x, co, qkv, ctx, lse, vec_rows, x_v, vt_v, send, recv, loc, *s):
    place = Place()
    enter(place)
    copies = Copies(send, recv, loc)
    mk = functools.partial(GatherPart, place, copies)
    n = shard.shape[1]
    third, half = n // 3, n // 2
    first = [
        mk(shard.at[0], g.at[0], P_Y, pl.ds(0, third)),
        mk(shard.at[0], g.at[0], P_Z, pl.ds(third, third)),
        mk(shard.at[0], g.at[0], P_X, pl.ds(2 * third, third)),
        mk(vec, vt_v, P_Y, pl.ds(0, vec.shape[0]), FEATURES),
    ]
    later = [
        mk(shard.at[1], g.at[1], P_Y, pl.ds(0, half)),
        mk(shard.at[1], g.at[1], P_Z, pl.ds(half, half)),
        mk(shard.at[2], g.at[2], P_Y, pl.ds(0, half)),
        mk(shard.at[2], g.at[2], P_Z, pl.ds(half, half)),
    ]
    for part in first:
        part.begin()
    rows = start_rows(place, copies, tok, x_v)
    for stage in range(4):
        for part in first:
            part.advance()
        if stage == 0:
            for part in later:
                part.begin()
    for part in first:
        part.finish()
    wait_all(rows)
    keep = copies.here(lambda: (x_v, x))
    moved = []

    def advance(parts):
        for part in parts:
            part.advance()

    def cot_rows():
        moved.extend(start_rows(place, copies, cot, co))

    ticks = [
        (0, lambda: advance(later)),
        (1, cot_rows),
        (4, lambda: advance(later)),
        (8, lambda: advance(later)),
    ]
    fwd_core(lambda t: g.at[0, t // 2, t % 2], x_v, vt_v, seg, qkv, ctx, lse, vec_rows, s, ticks)
    advance(later)
    for part in later:
        part.finish()
    wait_all(moved)
    keep()


def fwd_comm(shard, vec, tok, cot, seg):
    groups, block, width = tok.shape
    length = groups * block
    bits = (2,) * 5
    return pl.pallas_call(
        fwd_comm_kernel,
        in_specs=[ANY] * 4 + [VMEM],
        out_specs=[ANY] * 5 + [VMEM] * 2,
        out_shape=[
            jax.ShapeDtypeStruct((3,) + bits + shard.shape[1:], BF),
            jax.ShapeDtypeStruct(tok.shape, BF),
            jax.ShapeDtypeStruct(cot.shape, BF),
        ]
        + fwd_shapes(groups, length, width),
        scratch_shapes=[
            pltpu.VMEM(tok.shape, BF),
            pltpu.VMEM(bits + vec.shape, F32),
            *sems(80),
            pltpu.SemaphoreType.DMA((20,)),
        ]
        + fwd_scratch(groups, length, width),
        compiler_params=params(0),
        name="attention_forward",
    )(shard, vec, tok, cot, seg)


def fwd_plain_kernel(g, x, vt, seg, qkv, ctx, lse, vec_rows, sem, x_v, *s):
    copy = pltpu.make_async_copy(x, x_v, sem)
    copy.start()
    copy.wait()
    fwd_core(lambda t: g.at[0, t // 2, t % 2], x_v, vt, seg, qkv, ctx, lse, vec_rows, s, [])


def fwd_plain(g, x, vt, seg):
    groups, block, width = x.shape
    length = groups * block
    return pl.pallas_call(
        fwd_plain_kernel,
        in_specs=[ANY, ANY, VMEM, VMEM],
        out_specs=[ANY] * 2 + [VMEM] * 2,
        out_shape=fwd_shapes(groups, length, width),
        scratch_shapes=[pltpu.SemaphoreType.DMA, pltpu.VMEM(x.shape, BF)] + fwd_scratch(groups, length, width),
        compiler_params=params(),
        name="attention_forward",
    )(g, x, vt, seg)


def mid_kernel(g, x, cot, ctx, vec, out, grad, gh1, dctx, sums, x_v, cot_v, ctx_v, ao_v, in_v, dn_v, act_v, dact_v, dpre_v, y1_v, g2_v, out_v, gh1_v, dctx_v, t_v, sem, out_sem):
    groups, length = ctx.shape[:2]
    width = x.shape[2]
    half = width // 2
    blocks, block = x.shape[:2]

    def copy(src, dst, i):
        return pltpu.make_async_copy(src, dst, sem.at[i])

    loads = [copy(x, x_v, 0), copy(ctx, ctx_v, 1), copy(g.at[0, :, :, half:], ao_v, 2)]
    loads += [copy(g.at[1], in_v, 3), copy(g.at[2], dn_v, 4), copy(cot, cot_v, 5)]
    for load in loads:
        load.start()
    sums[...] = jnp.zeros_like(sums)
    for load in loads:
        load.wait()
    refs = (x_v, cot_v, ctx_v, ao_v, in_v, dn_v, vec, act_v, dact_v, dpre_v, y1_v, g2_v, out_v, gh1_v, dctx_v, sums)

    def step(i, carry):
        mid_rows(i, block, refs)
        pltpu.make_async_copy(out_v.at[i], out.at[i], out_sem.at[0, i]).start()
        pltpu.make_async_copy(gh1_v.at[i], gh1.at[i], out_sem.at[1, i]).start()
        return carry

    lax.fori_loop(0, blocks, step, 0)
    send = copy(dctx_v, dctx, 0)
    send.start()
    t_v[...] = y1_v[...].T

    def in_step(t, carry):
        in_v[t] = mm(t_v[...], dpre_v[t]).astype(BF)
        pltpu.make_async_copy(in_v.at[t], grad.at[0, t], out_sem.at[2, t]).start()
        return carry

    lax.fori_loop(0, groups, in_step, 0)
    t_v[...] = g2_v[...].T

    def dn_step(t, carry):
        dn_v[t] = mm(t_v[...], act_v[t]).astype(BF)
        pltpu.make_async_copy(dn_v.at[t], grad.at[1, t], out_sem.at[3, t]).start()
        return carry

    lax.fori_loop(0, groups, dn_step, 0)
    send.wait()
    for i in range(blocks):
        pltpu.make_async_copy(out_v.at[i], out.at[i], out_sem.at[0, i]).wait()
        pltpu.make_async_copy(gh1_v.at[i], gh1.at[i], out_sem.at[1, i]).wait()
    for t in range(groups):
        pltpu.make_async_copy(in_v.at[t], grad.at[0, t], out_sem.at[2, t]).wait()
        pltpu.make_async_copy(dn_v.at[t], grad.at[1, t], out_sem.at[3, t]).wait()


def middle(g, x, cot, ctx, vec):
    groups, length, _ = ctx.shape
    blocks, block, width = x.shape
    flats = (groups, width, width)
    return pl.pallas_call(
        mid_kernel,
        in_specs=[ANY] * 4 + [VMEM],
        out_specs=[ANY] * 4 + [VMEM],
        out_shape=[
            jax.ShapeDtypeStruct(x.shape, BF),
            jax.ShapeDtypeStruct((2,) + flats, BF),
            jax.ShapeDtypeStruct(x.shape, F32),
            jax.ShapeDtypeStruct(ctx.shape, BF),
            jax.ShapeDtypeStruct((8 + groups, 8, width), F32),
        ],
        scratch_shapes=[
            pltpu.VMEM(x.shape, BF),
            pltpu.VMEM(x.shape, BF),
            pltpu.VMEM(ctx.shape, BF),
            pltpu.VMEM((groups, width, width // 2), BF),
            pltpu.VMEM(flats, BF),
            pltpu.VMEM(flats, BF),
            pltpu.VMEM((groups, length, width), BF),
            pltpu.VMEM((groups, block, width), BF),
            pltpu.VMEM((groups, length, width), BF),
            pltpu.VMEM((length, width), BF),
            pltpu.VMEM((length, width), BF),
            pltpu.VMEM(x.shape, BF),
            pltpu.VMEM(x.shape, F32),
            pltpu.VMEM(ctx.shape, BF),
            pltpu.VMEM((width, length), BF),
            pltpu.SemaphoreType.DMA((6,)),
            pltpu.SemaphoreType.DMA((4, max(groups, blocks))),
        ],
        compiler_params=params(),
        name="feed_forward",
    )(g, x, cot, ctx, vec)


def bwd_core(qkv, ctx, dctx, lse, seg, dqkv, s, ticks):
    (qkv_v, ctx_v, dctx_v, oh_v, km_v, qa_v, ka_v, va_v, da_v, kt_v, dqt_v, out_v, in_sem, out_sem) = s
    groups, length = qkv.shape[:2]
    block = 256
    blocks = length // block

    def loads(t):
        slot = t % 2
        return [
            pltpu.make_async_copy(qkv.at[t], qkv_v.at[slot], in_sem.at[0, slot]),
            pltpu.make_async_copy(ctx.at[t], ctx_v.at[slot], in_sem.at[1, slot]),
            pltpu.make_async_copy(dctx.at[t], dctx_v.at[slot], in_sem.at[2, slot]),
        ]

    for load in loads(0):
        load.start()
    oh_v[...] = jnp.where(seg[...] == lane_ids(oh_v.shape) % HD, 1.0, 0.0).astype(BF)
    km_v[...] = key_marks(seg, km_v.shape)

    def step(i, carry):
        t, b = i // blocks, i % blocks
        slot = t % 2
        at_tick(i, ticks)

        @pl.when(b == 0)
        def _():
            for load in loads(t):
                load.wait()

            @pl.when(t + 1 < groups)
            def _():
                for load in loads(t + 1):
                    load.start()

            bwd_group(t, qkv_v.at[slot], ctx_v.at[slot], dctx_v.at[slot], lse, oh_v, km_v, qa_v, ka_v, va_v, da_v, kt_v, dqt_v)

        rows = pl.ds(pl.multiple_of(b * block, block), block)
        bwd_block(rows, block, qa_v, ka_v, va_v, da_v, kt_v, dqt_v, out_v.at[t])

        @pl.when(b == blocks - 1)
        def _():
            bwd_finish(dqt_v, out_v.at[t])
            pltpu.make_async_copy(out_v.at[t], dqkv.at[t], out_sem.at[t]).start()

        return carry

    lax.fori_loop(0, groups * blocks, step, 0)
    for t in range(groups):
        pltpu.make_async_copy(out_v.at[t], dqkv.at[t], out_sem.at[t]).wait()


def bwd_scratch(groups, length, width):
    half = 3 * LANES
    return [
        pltpu.VMEM((2, length, width), BF),
        pltpu.VMEM((2, length, half), BF),
        pltpu.VMEM((2, length, half), BF),
        pltpu.VMEM((length, LANES), BF),
        pltpu.VMEM((length, LANES), BF),
        pltpu.VMEM((3, length, LANES), BF),
        pltpu.VMEM((3, length, LANES), BF),
        pltpu.VMEM((3, length, LANES), BF),
        pltpu.VMEM((3, length, LANES), BF),
        pltpu.VMEM((2, LANES, length), BF),
        pltpu.VMEM((2, LANES, length), F32),
        pltpu.VMEM((groups, length, width), BF),
        pltpu.SemaphoreType.DMA((3, 2)),
        pltpu.SemaphoreType.DMA((groups,)),
    ]


def bwd_comm_kernel(qkv, ctx, dctx, lse, seg, grad, out, dqkv, own, out_rows, total, r0, r1, r2, r3, r4, r5, r6, r7, r8, r9, send, recv, loc, *s):
    place = Place()
    enter(place)
    copies = Copies(send, recv, loc)
    n = own.shape[1]
    half = n // 2
    arrive = ((r0, r1, r2, r3, r4), (r5, r6, r7, r8, r9))
    parts = []
    for w in range(2):
        for i, order in enumerate((P_Y, P_Z)):
            rows = pl.ds(i * half, half)
            parts.append(ReducePart(place, copies, grad.at[w], total.at[w], arrive[w], own.at[w], order[::-1], rows))
    for part in parts:
        part.begin()
    moved = []

    def advance():
        for part in parts:
            part.advance()

    def rows():
        moved.extend(start_rows(place, copies, out, out_rows))

    ticks = [(1, advance), (2, rows), (6, advance), (9, advance), (12, advance), (15, advance)]
    bwd_core(qkv, ctx, dctx, lse, seg, dqkv, s, ticks)
    wait_all(moved)


def bwd_comm(qkv, ctx, dctx, lse, seg, grad, out):
    groups, length, width = qkv.shape
    n = grad.shape[6]
    arrive = arrivals(n, width, BF)
    return pl.pallas_call(
        bwd_comm_kernel,
        in_specs=[ANY] * 3 + [VMEM] * 2 + [ANY] * 2,
        out_specs=[ANY, VMEM, ANY],
        out_shape=[
            jax.ShapeDtypeStruct(qkv.shape, BF),
            jax.ShapeDtypeStruct((2, n, width), F32),
            jax.ShapeDtypeStruct(out.shape, BF),
        ],
        scratch_shapes=[
            pltpu.VMEM((2, 2, 2, 2, 2, n, width), BF),
            *arrive,
            *arrive,
            *sems(40),
            pltpu.SemaphoreType.DMA((10,)),
        ]
        + bwd_scratch(groups, length, width),
        compiler_params=params(1),
        name="attention_backward",
    )(qkv, ctx, dctx, lse, seg, grad, out)


def bwd_plain_kernel(qkv, ctx, dctx, lse, seg, dqkv, *s):
    bwd_core(qkv, ctx, dctx, lse, seg, dqkv, s, [])


def bwd_plain(qkv, ctx, dctx, lse, seg):
    groups, length, width = qkv.shape
    return pl.pallas_call(
        bwd_plain_kernel,
        in_specs=[ANY] * 3 + [VMEM] * 2,
        out_specs=ANY,
        out_shape=jax.ShapeDtypeStruct(qkv.shape, BF),
        scratch_shapes=bwd_scratch(groups, length, width),
        compiler_params=params(),
        name="attention_backward",
    )(qkv, ctx, dctx, lse, seg)


def end_loads(g, x, ctx, gh1, dqkv, refs, sem):
    a_v, x_v, ctx_v, gh1_v, dqkv_v = refs
    pairs = ((x, x_v), (gh1, gh1_v), (ctx, ctx_v), (dqkv, dqkv_v), (g.at[0], a_v))
    copies = [pltpu.make_async_copy(src, dst, sem.at[i]) for i, (src, dst) in enumerate(pairs)]
    for copy in copies:
        copy.start()
    return copies


def end_turn(x_v, gh1_v, xt_v, gt_v):
    xt_v[...] = flat(x_v[...]).T
    gt_v[...] = flat(gh1_v[...]).astype(BF).T


def end_group(t, xt_v, gt_v, ctx_v, dqkv_v, da_v, qsum_v):
    half = 3 * LANES
    d = dqkv_v[t]
    lead = d[:, :half]
    rest = d[:, half:]
    whole = da_v.reshape(dqkv_v.shape[0], *xt_v.shape[:1], d.shape[1])
    whole[t, :, :half] = mm(xt_v[...], lead).astype(BF)
    rest = mm(xt_v[...], rest) + mm(gt_v[...], ctx_v[t])
    whole[t, :, half:] = rest.astype(BF)
    qsum_v[t] = mm(jnp.ones((8, d.shape[0]), BF), d)


def end_rows(r, block, gh1_v, dqkv_v, a_v, gx_v):
    rows = pl.ds(pl.multiple_of(r * block, block), block)
    total = gh1_v[r]
    for t in range(dqkv_v.shape[0]):
        total = total + mm(dqkv_v[t, rows, :], a_v[t], NT)
    gx_v[r] = total.astype(BF)


def end_vectors(sums, qsum_v, tab_v):
    groups = qsum_v.shape[0]
    tab_v[...] = jnp.zeros_like(tab_v)
    for t in range(groups):
        tab_v[t : t + 1, :] = qsum_v[t][:1]
    parts = tab_v[...].T
    for k in range(sums.shape[0]):
        tab_v[k : k + 1, :] = jnp.sum(sums[k], axis=0, keepdims=True)
    table = tab_v[...].T
    q, v = [], []
    for t in range(groups):
        col = parts[:, t : t + 1]
        q += [col[:LANES], col[3 * LANES : 3 * LANES + HD]]
        v += [col[2 * LANES : 3 * LANES], col[5 * LANES : 5 * LANES + HD]]
    lanes = lane_ids(table.shape)
    table = jnp.where(lanes == 6, jnp.concatenate(q, axis=0), table)
    table = jnp.where(lanes == 7, jnp.concatenate(v, axis=0), table)
    return table


def sum_comm_kernel(da, vt, gx, own, vec_own, gx_rows, total, vtot, r0, r1, r2, r3, r4, r5, r6, r7, r8, r9, send, recv, loc):
    place = Place()
    enter(place)
    copies = Copies(send, recv, loc)
    third = own.shape[0] // 3
    parts = []
    for i, order in enumerate((P_Y, P_Z, P_X)):
        rows = pl.ds(i * third, third)
        parts.append(ReducePart(place, copies, da, total, (r0, r1, r2, r3, r4), own, order[::-1], rows))
    rows = pl.ds(0, vec_own.shape[0])
    parts.append(ReducePart(place, copies, vt, vtot, (r5, r6, r7, r8, r9), vec_own, P_Y[::-1], rows, FEATURES))
    for part in parts:
        part.begin()
    moved = start_rows(place, copies, gx, gx_rows)
    for stage in range(5):
        for part in parts:
            part.advance()
    wait_all(moved)


def end_scratch(x, ctx, dqkv, width):
    groups, length, _ = dqkv.shape
    return [
        pltpu.VMEM((groups, width, width), BF),
        pltpu.VMEM(x.shape, BF),
        pltpu.VMEM(ctx.shape, BF),
        pltpu.VMEM(x.shape, F32),
        pltpu.VMEM(dqkv.shape, BF),
        pltpu.VMEM((width, length), BF),
        pltpu.VMEM((width, length), BF),
        pltpu.VMEM((2,) * 5 + (width // 8, width), BF),
        pltpu.VMEM((groups, 8, width), F32),
        pltpu.VMEM(x.shape, BF),
        pltpu.VMEM((LANES, width), F32),
    ]


def sum_comm(da, vt, gx):
    n, width = da.shape[-2:]
    fine = vt.shape[-2]
    return pl.pallas_call(
        sum_comm_kernel,
        in_specs=[ANY] * 3,
        out_specs=[VMEM, VMEM, ANY],
        out_shape=[
            jax.ShapeDtypeStruct((n, width), F32),
            jax.ShapeDtypeStruct((fine, LANES), F32),
            jax.ShapeDtypeStruct(gx.shape, BF),
        ],
        scratch_shapes=[
            pltpu.VMEM((2,) * 4 + (n, width), BF),
            pltpu.VMEM((2,) * 4 + (fine, LANES), F32),
            *arrivals(n, width, BF),
            *arrivals(fine, LANES, F32),
            *sems(40),
            pltpu.SemaphoreType.DMA((10,)),
        ],
        compiler_params=params(2),
        name="weight_sums",
    )(da, vt, gx)


def end_plain_kernel(g, x, ctx, gh1, dqkv, sums, da, vt, gx, a_v, x_v, ctx_v, gh1_v, dqkv_v, xt_v, gt_v, da_v, qsum_v, gx_v, tab_v, load_sem, out_sem):
    loads = end_loads(g, x, ctx, gh1, dqkv, (a_v, x_v, ctx_v, gh1_v, dqkv_v), load_sem)
    for load in loads:
        load.wait()
    end_turn(x_v, gh1_v, xt_v, gt_v)

    def group(t, carry):
        end_group(t, xt_v, gt_v, ctx_v, dqkv_v, da_v, qsum_v)
        return carry

    lax.fori_loop(0, dqkv_v.shape[0], group, 0)
    block = gx_v.shape[1]

    def rows(r, carry):
        end_rows(r, block, gh1_v, dqkv_v, a_v, gx_v)
        return carry

    lax.fori_loop(0, gx_v.shape[0], rows, 0)
    vt[...] = end_vectors(sums, qsum_v, tab_v)
    copies = [pltpu.make_async_copy(da_v, da, out_sem.at[0]), pltpu.make_async_copy(gx_v, gx, out_sem.at[1])]
    for copy in copies:
        copy.start()
    for copy in copies:
        copy.wait()


def end_plain(g, x, ctx, gh1, dqkv, sums):
    width = x.shape[2]
    return pl.pallas_call(
        end_plain_kernel,
        in_specs=[ANY] * 5 + [VMEM],
        out_specs=[ANY, VMEM, ANY],
        out_shape=[
            jax.ShapeDtypeStruct((2,) * 5 + (width // 8, width), BF),
            jax.ShapeDtypeStruct((width, LANES), F32),
            jax.ShapeDtypeStruct(x.shape, BF),
        ],
        scratch_shapes=end_scratch(x, ctx, dqkv, width) + [pltpu.SemaphoreType.DMA((5,)), pltpu.SemaphoreType.DMA((2,))],
        compiler_params=params(),
        name="weight_gradients",
    )(g, x, ctx, gh1, dqkv, sums)


def pack(qkv_weight, out_weight, in_weight, down_weight):
    q, k, v = qkv_weight[0], qkv_weight[1], qkv_weight[2]
    o = out_weight.T
    a = [q[:, :LANES], k[:, :LANES], v[:, :LANES]]
    a += [q[:, LANES:], o[:, HD:LANES], k[:, LANES:], o[:, :HD], v[:, LANES:], o[:, LANES:]]
    return jnp.stack([jnp.concatenate(a, axis=1), in_weight, down_weight.T])


def unpack(a):
    def cut(i, half):
        start = i * LANES + half * HD
        return a[:, start : start + HD]

    heads = [jnp.concatenate([cut(i, 0), cut(i, 1), cut(3 + i, 0)], axis=1) for i in range(3)]
    out = jnp.concatenate([cut(4, 1), cut(3, 1), cut(5, 1)], axis=1)
    return jnp.stack(heads), out.T


def local(tokens, segments, qkv_weight, out_weight, in_weight, down_weight, vectors, cotangent):
    n_dp, n_t = lax.axis_size("dp"), lax.axis_size("tensor")
    groups, block, width = tokens.shape
    length = groups * block
    n = in_weight.shape[0]
    fine = vectors.shape[1]
    n_v = vectors.shape[0]
    seg = lax.dynamic_slice_in_dim(segments, lax.axis_index("tensor"), 1, 0).reshape(length, 1)
    shard = pack(qkv_weight, out_weight, in_weight, down_weight)
    vec = jnp.pad(vectors.T, ((0, 0), (0, LANES - n_v)))
    kernels = n_dp == 8 and n_t == 4
    bits = (2,) * 5
    if kernels:
        g, x, cot, qkv, ctx, lse, rows = fwd_comm(shard, vec, tokens, cotangent, seg)
    else:
        full = lax.all_gather(shard, ALL, axis=0, tiled=False).reshape(n_dp, n_t, 3, n, width)
        g = full.transpose(2, 1, 0, 3, 4).reshape((3,) + bits + (width // 8, width))
        vt = lax.all_gather(vec, ALL, axis=0, tiled=True)
        x = lax.all_to_all(tokens, "tensor", split_axis=0, concat_axis=0, tiled=True)
        cot = lax.all_to_all(cotangent, "tensor", split_axis=0, concat_axis=0, tiled=True)
        qkv, ctx, lse, rows = fwd_plain(g, x, vt, seg)
    g = g.reshape(3, groups, width, width)
    out, grad, gh1, dctx, sums = middle(g, x, cot, ctx, rows)
    if kernels:
        grad = grad.reshape((2,) + bits + (n, width))
        dqkv, own, out_rows = bwd_comm(qkv, ctx, dctx, lse, seg, grad, out)
        da, vt, gx = end_plain(g, x, ctx, gh1, dqkv, sums)
        own_a, own_v, gx_rows = sum_comm(da, vt.reshape(bits + (fine, LANES)), gx)
    else:
        dqkv = bwd_plain(qkv, ctx, dctx, lse, seg)
        da, vt, gx = end_plain(g, x, ctx, gh1, dqkv, sums)
        every_grad = jnp.concatenate([da.reshape(1, n_t, n_dp, n, width), grad.reshape(2, n_t, n_dp, n, width)])
        every_grad = every_grad.transpose(2, 1, 0, 3, 4).reshape(n_dp * n_t, 3, n, width)
        own = lax.psum_scatter(every_grad, ALL, scatter_dimension=0, tiled=True)[0].astype(F32)
        own_a, own = own[0], own[1:]
        own_v = lax.psum_scatter(vt[:, :n_v], ALL, scatter_dimension=0, tiled=True)
        out_rows = lax.all_to_all(out, "tensor", split_axis=0, concat_axis=0, tiled=True)
        gx_rows = lax.all_to_all(gx, "tensor", split_axis=0, concat_axis=0, tiled=True)
    d_qkv, d_out = unpack(own_a)
    return out_rows, gx_rows, d_qkv, d_out, own[0], own[1].T, own_v[:, :n_v].T


def solution(mesh):
    rows = P("dp", "tensor", None)
    weights = (P(None, "dp", "tensor"), P("tensor", "dp"), P("dp", "tensor"), P("tensor", "dp"), P(None, ("dp", "tensor")))
    in_specs = (rows, P("dp", None), *weights, rows)
    out_specs = (rows, rows, *weights)
    return jax.shard_map(local, mesh=mesh, in_specs=in_specs, out_specs=out_specs, check_vma=False)
```

profile of v0, /device:TPU:0, one launch (start us, length us, event | category | flops | bytes accessed | tf_op | source)
XLA Modules:
  0.0 340.9 jit_solution(15142180549499785539)
XLA Ops:
  0.7 0.7 copy-done
  1.4 0.8 copy.20
  2.1 0.6 pad.4.vec
  2.8 0.9 copy.19
  3.7 0.9 slice_bitcast_fusion.2
  4.7 0.1 concatenate.18
  4.8 1.8 pad_maximum_fusion.shard
  6.6 1.0 copy.21.seg
  7.6 111.9 %attention_forward.1 = (bf16[3,2,2,2,2,2,96,768]{7,6,5,4,3,2,1,0:T(8,128)(2,1)}, bf16[4,256,768]{2,1,0:T(8,128)(2,1)}, bf16[4,256,768]{2,1,0:T(8,128)(2,1)}, bf1...) custom-call(bf16[3,96,768]{2,1,0:T(8,128)(2,1)} %pad_maximum_fusion.shard, ...), custom_call_target="tpu_custom_call" | custom-call | tf_op jit(solution)/shard_map/attention_forward/pallas_call | solution.py:688
  119.5 62.1 %feed_forward.1 = (bf16[4,256,768]{2,1,0:T(8,128)(2,1)}, bf16[2,4,768,768]{3,2,1,0:T(8,128)(2,1)}, f32[4,256,768]{2,1,0:T(8,128)}, bf16[4,1024,384]{2,1,0:T(8,128)(2,1)}, f32[12,8,768]{2,1,0:T(8,128)}) custom-call(bf16[3,4,768,768]{3,2,1,0:T(8,128)(2,1)} %bitcast.34, bf16[4,256,768]{2,1,0:T(8,128)(2,1)} %get-tuple-element.31.x, ...), custom_call_target="tpu_custom_call" | custom-call | tf_op jit(solution)/shard_map/feed_forward/pallas_call | solution.py:787
  181.6 77.0 %attention_backward.1 = (bf16[4,1024,768]{2,1,0:T(8,128)(2,1)}, f32[2,96,768]{2,1,0:T(8,128)}, bf16[4,256,768]{2,1,0:T(8,128)(2,1)}) custom-call(bf16[4,1024,768]{2,1,0:T(8,128)(2,1)} %get-tuple-element.28.qkv, bf16[4,1024,384]{2,1,0:T(8,128)(2,1)} %get-tuple-element.29.ctx, bf16[4,1024,384]{2,1,0:T(8,128)(2,1)} %get-tuple-element.34.dctx, ...), custom_call_target="tpu_custom_call" | custom-call | tf_op jit(solution)/shard_map/attention_backward/pallas_call | solution.py:925
  258.6 27.3 %weight_gradients.1 = (bf16[2,2,2,2,2,96,768]{6,5,4,3,2,1,0:T(8,128)(2,1)}, f32[768,128]{1,0:T(8,128)}, bf16[4,256,768]{2,1,0:T(8,128)(2,1)}) custom-call(bf16[3,4,768,768]{3,2,1,0:T(8,128)(2,1)} %bitcast.35, bf16[4,256,768]{2,1,0:T(8,128)(2,1)} %get-tuple-element.31.x, bf16[4,1024,384]{2,1,0:T(8,128)(2,1)} %get-tuple-element.29.ctx, ...), custom_call_target="tpu_custom_call" | custom-call | tf_op jit(solution)/shard_map/weight_gradients/pallas_call | solution.py:1108
  285.9 46.0 %weight_sums.1 = (f32[96,768]{1,0:T(8,128)}, f32[24,128]{1,0:T(8,128)}, bf16[4,256,768]{2,1,0:T(8,128)(2,1)}) custom-call(bf16[2,2,2,2,2,96,768]{6,5,4,3,2,1,0:T(8,128)(2,1)} %get-tuple-element.42.da, f32[2,2,2,2,2,24,128]{6,5,4,3,2,1,0:T(8,128)} %bitcast.38, bf16[4,256,768]{2,1,0:T(8,128)(2,1)} %get-tuple-element.44.gx), custom_call_target="tpu_custom_call" | custom-call | tf_op jit(solution)/shard_map/weight_sums/pallas_call | solution.py:1058
  331.9 0.8 slice_bitcast_fusion.5
  332.6 0.7 copy.24
  333.3 0.9 fusion.1
  334.2 1.1 fusion
  335.3 0.1 maximum_bitcast_fusion.3
  335.4 0.7 copy.23
  336.2 0.7 pad_maximum_fusion.1
  336.9 0.8 slice_bitcast_fusion
  337.8 1.1 copy.27
  338.9 0.8 copy-done.3
  339.8 1.1 copy.28
  (18 shorter events, 0.2 us)
Async XLA Ops:
  0.6 0.7 copy-start
  331.9 5.1 %copy-start.4 = (f32[2,96,768]{2,1,0:T(8,128)S(1)}, f32[2,96,768]{2,1,0:T(8,128)}, u32[]{:S(2)}) copy-start(f32[2,96,768]{2,1,0:T(8,128)} %get-tuple-element.47) | copy-start | bytes 1769476
  334.2 3.6 %copy-start.2 = (bf16[4,256,768]{2,1,0:T(8,128)(2,1)S(1)}, bf16[4,256,768]{2,1,0:T(8,128)(2,1)}, u32[]{:S(2)}) copy-start(bf16[4,256,768]{2,1,0:T(8,128)(2,1)} %get-tuple-element.89) | copy-start | bytes 4718596
  337.8 2.0 copy-start.3
  337.8 3.1 copy-start.1
where the time goes:
time: 342 us; the launch traced here: 341 us
  Pallas kernels  324 us (95%)
  local copies, waits for them, and re-layouts  13.2 us (4%)
    pallas_call x1, Pallas kernels, fwd_comm(): pl.pallas_call(fwd_comm_kernel, in_specs=[ANY] * 4 + [VMEM], out_specs=[A...  112 us
    pallas_call x1, Pallas kernels, bwd_comm(): pl.pallas_call(bwd_comm_kernel, in_specs=[ANY] * 3 + [VMEM] * 2 + [ANY] *...  77 us
    pallas_call x1, Pallas kernels, middle(): pl.pallas_call(mid_kernel, in_specs=[ANY] * 4 + [VMEM], out_specs=[ANY] *...  62.1 us
    pallas_call x1, Pallas kernels, sum_comm(): pl.pallas_call(sum_comm_kernel, in_specs=[ANY] * 3, out_specs=[VMEM, VMEM...  46 us
    pallas_call x1, Pallas kernels, end_plain(): pl.pallas_call(end_plain_kernel, in_specs=[ANY] * 5 + [VMEM], out_specs=[...  27.3 us
    unnamed x16, local copies, waits for them, and re-layouts  6.92 us

commit v1 on v0

--- a/solution.py
+++ b/solution.py
@@ -299,7 +299,10 @@
 FEATURES = ("z2", "z1", "y", "x", "c")
 P_Y = ("z2", "z1", "x", "y")
 P_Z = ("z2", "x", "y", "z1")
-P_X = ("z2", "y", "z1", "x")
+Q_Y = ("z2", "x", "z1", "y")
+Q_Z = ("z2", "x", "y", "z1")
+Q_X = ("x", "z2", "z1", "y")
+Q_M = ("y", "z2", "x", "z1")
 
 
 class Place:
@@ -634,47 +637,49 @@
     n = shard.shape[1]
     third, half = n // 3, n // 2
     first = [
-        mk(shard.at[0], g.at[0], P_Y, pl.ds(0, third)),
-        mk(shard.at[0], g.at[0], P_Z, pl.ds(third, third)),
-        mk(shard.at[0], g.at[0], P_X, pl.ds(2 * third, third)),
-        mk(vec, vt_v, P_Y, pl.ds(0, vec.shape[0]), FEATURES),
+        mk(shard.at[0], g.at[0], Q_X, pl.ds(0, third)),
+        mk(shard.at[0], g.at[0], Q_Y, pl.ds(third, third)),
+        mk(shard.at[0], g.at[0], Q_Z, pl.ds(2 * third, third)),
+        mk(vec, vt_v, Q_Y, pl.ds(0, vec.shape[0]), FEATURES),
     ]
     later = [
-        mk(shard.at[1], g.at[1], P_Y, pl.ds(0, half)),
-        mk(shard.at[1], g.at[1], P_Z, pl.ds(half, half)),
-        mk(shard.at[2], g.at[2], P_Y, pl.ds(0, half)),
-        mk(shard.at[2], g.at[2], P_Z, pl.ds(half, half)),
+        mk(shard.at[1], g.at[1], Q_Y, pl.ds(0, half)),
+        mk(shard.at[1], g.at[1], Q_Z, pl.ds(half, half)),
+        mk(shard.at[2], g.at[2], Q_M, pl.ds(0, half)),
+        mk(shard.at[2], g.at[2], Q_Y, pl.ds(half, half)),
     ]
+    moved = []
+
+    def advance(*which):
+        for i in which:
+            later[i].advance()
+
+    def cot_rows():
+        moved.extend(start_rows(place, copies, cot, co))
+
     for part in first:
         part.begin()
     rows = start_rows(place, copies, tok, x_v)
     for stage in range(4):
         for part in first:
             part.advance()
-        if stage == 0:
+        if stage == 1:
             for part in later:
                 part.begin()
+        if stage > 1:
+            advance(0, 1, 2, 3)
     for part in first:
         part.finish()
     wait_all(rows)
     keep = copies.here(lambda: (x_v, x))
-    moved = []
-
-    def advance(parts):
-        for part in parts:
-            part.advance()
-
-    def cot_rows():
-        moved.extend(start_rows(place, copies, cot, co))
-
     ticks = [
-        (0, lambda: advance(later)),
-        (1, cot_rows),
-        (4, lambda: advance(later)),
-        (8, lambda: advance(later)),
+        (0, cot_rows),
+        (4, functools.partial(advance, 1)),
+        (7, functools.partial(advance, 0, 2, 3)),
+        (15, functools.partial(advance, 1)),
     ]
     fwd_core(lambda t: g.at[0, t // 2, t % 2], x_v, vt_v, seg, qkv, ctx, lse, vec_rows, s, ticks)
-    advance(later)
+    advance(2, 0, 3)
     for part in later:
         part.finish()
     wait_all(moved)
@@ -819,11 +824,12 @@
     )(g, x, cot, ctx, vec)
 
 
-def bwd_core(qkv, ctx, dctx, lse, seg, dqkv, s, ticks):
-    (qkv_v, ctx_v, dctx_v, oh_v, km_v, qa_v, ka_v, va_v, da_v, kt_v, dqt_v, out_v, in_sem, out_sem) = s
+def bwd_core(qkv, ctx, dctx, lse, seg, x, gh1, g, da, gx, qsum, s, ticks):
+    (qkv_v, ctx_v, dctx_v, a_v, oh_v, km_v, qa_v, ka_v, va_v, da_v, kt_v, dqt_v, dqkv_v, x_v, gx_v, xt_v, gt_v, dw_v, in_sem, out_sem, x_sem) = s
     groups, length = qkv.shape[:2]
     block = 256
     blocks = length // block
+    half = 3 * LANES
 
     def loads(t):
         slot = t % 2
@@ -831,12 +837,35 @@
             pltpu.make_async_copy(qkv.at[t], qkv_v.at[slot], in_sem.at[0, slot]),
             pltpu.make_async_copy(ctx.at[t], ctx_v.at[slot], in_sem.at[1, slot]),
             pltpu.make_async_copy(dctx.at[t], dctx_v.at[slot], in_sem.at[2, slot]),
+            pltpu.make_async_copy(g.at[0, t], a_v.at[slot], in_sem.at[3, slot]),
         ]
 
-    for load in loads(0):
+    def result(t):
+        return pltpu.make_async_copy(dw_v.at[t], da.at[t], out_sem.at[t])
+
+    more = [pltpu.make_async_copy(x, x_v, x_sem.at[0]), pltpu.make_async_copy(gh1, gx_v, x_sem.at[1])]
+    for load in loads(0) + more:
         load.start()
     oh_v[...] = jnp.where(seg[...] == lane_ids(oh_v.shape) % HD, 1.0, 0.0).astype(BF)
     km_v[...] = key_marks(seg, km_v.shape)
+    for load in more:
+        load.wait()
+    xt_v[...] = flat(x_v[...]).T
+    gt_v[...] = flat(gx_v[...]).astype(BF).T
+
+    def weights(t, slot):
+        def chunk(r, inner):
+            part = pl.ds(pl.multiple_of(r * block, block), block)
+            dw_v[t, part, :half] = mm(xt_v[part, :], dqkv_v[:, :half]).astype(BF)
+            dw_v[t, part, half:] = (mm(xt_v[part, :], dqkv_v[:, half:]) + mm(gt_v[part, :], ctx_v[slot])).astype(BF)
+            return inner
+
+        lax.fori_loop(0, dw_v.shape[1] // block, chunk, 0)
+        qsum[t] = mm(jnp.ones((8, length), BF), dqkv_v[...])
+
+    def rows(b, slot):
+        part = pl.ds(pl.multiple_of(b * block, block), block)
+        gx_v[b] = gx_v[b] + mm(dqkv_v[part, :], a_v[slot], NT)
 
     def step(i, carry):
         t, b = i // blocks, i % blocks
@@ -855,27 +884,44 @@
 
             bwd_group(t, qkv_v.at[slot], ctx_v.at[slot], dctx_v.at[slot], lse, oh_v, km_v, qa_v, ka_v, va_v, da_v, kt_v, dqt_v)
 
-        rows = pl.ds(pl.multiple_of(b * block, block), block)
-        bwd_block(rows, block, qa_v, ka_v, va_v, da_v, kt_v, dqt_v, out_v.at[t])
+        part = pl.ds(pl.multiple_of(b * block, block), block)
+        bwd_block(part, block, qa_v, ka_v, va_v, da_v, kt_v, dqt_v, dqkv_v)
 
         @pl.when(b == blocks - 1)
         def _():
-            bwd_finish(dqt_v, out_v.at[t])
-            pltpu.make_async_copy(out_v.at[t], dqkv.at[t], out_sem.at[t]).start()
+            bwd_finish(dqt_v, dqkv_v)
+            weights(t, slot)
+            result(t).start()
+
+            def row_step(r, inner):
+                rows(r, slot)
+                return inner
+
+            lax.fori_loop(0, blocks, row_step, 0)
 
         return carry
 
     lax.fori_loop(0, groups * blocks, step, 0)
+
+    def low_step(r, carry):
+        x_v[r] = gx_v[r].astype(BF)
+        return carry
+
+    lax.fori_loop(0, blocks, low_step, 0)
+    last = pltpu.make_async_copy(x_v, gx, x_sem.at[0])
+    last.start()
     for t in range(groups):
-        pltpu.make_async_copy(out_v.at[t], dqkv.at[t], out_sem.at[t]).wait()
-
-
-def bwd_scratch(groups, length, width):
+        result(t).wait()
+    last.wait()
+
+
+def bwd_scratch(groups, length, width, x):
     half = 3 * LANES
     return [
         pltpu.VMEM((2, length, width), BF),
         pltpu.VMEM((2, length, half), BF),
         pltpu.VMEM((2, length, half), BF),
+        pltpu.VMEM((2, width, width), BF),
         pltpu.VMEM((length, LANES), BF),
         pltpu.VMEM((length, LANES), BF),
         pltpu.VMEM((3, length, LANES), BF),
@@ -884,50 +930,72 @@
         pltpu.VMEM((3, length, LANES), BF),
         pltpu.VMEM((2, LANES, length), BF),
         pltpu.VMEM((2, LANES, length), F32),
-        pltpu.VMEM((groups, length, width), BF),
-        pltpu.SemaphoreType.DMA((3, 2)),
+        pltpu.VMEM((length, width), BF),
+        pltpu.VMEM(x, BF),
+        pltpu.VMEM(x, F32),
+        pltpu.VMEM((width, length), BF),
+        pltpu.VMEM((width, length), BF),
+        pltpu.VMEM((groups, width, width), BF),
+        pltpu.SemaphoreType.DMA((4, 2)),
         pltpu.SemaphoreType.DMA((groups,)),
+        pltpu.SemaphoreType.DMA((2,)),
     ]
 
 
-def bwd_comm_kernel(qkv, ctx, dctx, lse, seg, grad, out, dqkv, own, out_rows, total, r0, r1, r2, r3, r4, r5, r6, r7, r8, r9, send, recv, loc, *s):
+def bwd_shapes(groups, width, x):
+    return [
+        jax.ShapeDtypeStruct((groups, width, width), BF),
+        jax.ShapeDtypeStruct(x, BF),
+        jax.ShapeDtypeStruct((groups, 8, width), F32),
+    ]
+
+
+def bwd_comm_kernel(qkv, ctx, dctx, lse, seg, x, gh1, g, grad, out, da, gx, qsum, own, out_rows, total, r0, r1, r2, r3, r4, r5, r6, r7, r8, r9, send, recv, loc, *s):
     place = Place()
     enter(place)
     copies = Copies(send, recv, loc)
-    n = own.shape[1]
-    half = n // 2
+    half = own.shape[1] // 2
     arrive = ((r0, r1, r2, r3, r4), (r5, r6, r7, r8, r9))
     parts = []
-    for w in range(2):
-        for i, order in enumerate((P_Y, P_Z)):
+    for w, orders in enumerate(((P_Y, P_Z), (Q_Y, Q_Z))):
+        for i, order in enumerate(orders):
             rows = pl.ds(i * half, half)
             parts.append(ReducePart(place, copies, grad.at[w], total.at[w], arrive[w], own.at[w], order[::-1], rows))
     for part in parts:
         part.begin()
     moved = []
 
-    def advance():
-        for part in parts:
-            part.advance()
+    def advance(*which):
+        for i in which:
+            parts[i].advance()
 
     def rows():
         moved.extend(start_rows(place, copies, out, out_rows))
 
-    ticks = [(1, advance), (2, rows), (6, advance), (9, advance), (12, advance), (15, advance)]
-    bwd_core(qkv, ctx, dctx, lse, seg, dqkv, s, ticks)
+    ticks = [
+        (2, functools.partial(advance, 0, 1, 2, 3)),
+        (3, rows),
+        (9, functools.partial(advance, 0, 1, 2, 3)),
+        (12, functools.partial(advance, 0, 2)),
+        (13, functools.partial(advance, 1, 3)),
+        (14, functools.partial(advance, 0, 2)),
+        (15, functools.partial(advance, 1, 3)),
+    ]
+    bwd_core(qkv, ctx, dctx, lse, seg, x, gh1, g, da, gx, qsum, s, ticks)
+    advance(0, 1, 2, 3)
     wait_all(moved)
 
 
-def bwd_comm(qkv, ctx, dctx, lse, seg, grad, out):
+def bwd_comm(qkv, ctx, dctx, lse, seg, x, gh1, g, grad, out):
     groups, length, width = qkv.shape
     n = grad.shape[6]
     arrive = arrivals(n, width, BF)
     return pl.pallas_call(
         bwd_comm_kernel,
-        in_specs=[ANY] * 3 + [VMEM] * 2 + [ANY] * 2,
-        out_specs=[ANY, VMEM, ANY],
-        out_shape=[
-            jax.ShapeDtypeStruct(qkv.shape, BF),
+        in_specs=[ANY] * 3 + [VMEM] * 2 + [ANY] * 5,
+        out_specs=[ANY, ANY, VMEM, VMEM, ANY],
+        out_shape=bwd_shapes(groups, width, x.shape)
+        + [
             jax.ShapeDtypeStruct((2, n, width), F32),
             jax.ShapeDtypeStruct(out.shape, BF),
         ],
@@ -938,61 +1006,27 @@
             *sems(40),
             pltpu.SemaphoreType.DMA((10,)),
         ]
-        + bwd_scratch(groups, length, width),
+        + bwd_scratch(groups, length, width, x.shape),
         compiler_params=params(1),
         name="attention_backward",
-    )(qkv, ctx, dctx, lse, seg, grad, out)
-
-
-def bwd_plain_kernel(qkv, ctx, dctx, lse, seg, dqkv, *s):
-    bwd_core(qkv, ctx, dctx, lse, seg, dqkv, s, [])
-
-
-def bwd_plain(qkv, ctx, dctx, lse, seg):
+    )(qkv, ctx, dctx, lse, seg, x, gh1, g, grad, out)
+
+
+def bwd_plain_kernel(qkv, ctx, dctx, lse, seg, x, gh1, g, da, gx, qsum, *s):
+    bwd_core(qkv, ctx, dctx, lse, seg, x, gh1, g, da, gx, qsum, s, [])
+
+
+def bwd_plain(qkv, ctx, dctx, lse, seg, x, gh1, g):
     groups, length, width = qkv.shape
     return pl.pallas_call(
         bwd_plain_kernel,
-        in_specs=[ANY] * 3 + [VMEM] * 2,
-        out_specs=ANY,
-        out_shape=jax.ShapeDtypeStruct(qkv.shape, BF),
-        scratch_shapes=bwd_scratch(groups, length, width),
+        in_specs=[ANY] * 3 + [VMEM] * 2 + [ANY] * 3,
+        out_specs=[ANY, ANY, VMEM],
+        out_shape=bwd_shapes(groups, width, x.shape),
+        scratch_shapes=bwd_scratch(groups, length, width, x.shape),
         compiler_params=params(),
         name="attention_backward",
-    )(qkv, ctx, dctx, lse, seg)
-
-
-def end_loads(g, x, ctx, gh1, dqkv, refs, sem):
-    a_v, x_v, ctx_v, gh1_v, dqkv_v = refs
-    pairs = ((x, x_v), (gh1, gh1_v), (ctx, ctx_v), (dqkv, dqkv_v), (g.at[0], a_v))
-    copies = [pltpu.make_async_copy(src, dst, sem.at[i]) for i, (src, dst) in enumerate(pairs)]
-    for copy in copies:
-        copy.start()
-    return copies
-
-
-def end_turn(x_v, gh1_v, xt_v, gt_v):
-    xt_v[...] = flat(x_v[...]).T
-    gt_v[...] = flat(gh1_v[...]).astype(BF).T
-
-
-def end_group(t, xt_v, gt_v, ctx_v, dqkv_v, da_v, qsum_v):
-    half = 3 * LANES
-    d = dqkv_v[t]
-    lead = d[:, :half]
-    rest = d[:, half:]
-    whole = da_v.reshape(dqkv_v.shape[0], *xt_v.shape[:1], d.shape[1])
-    whole[t, :, :half] = mm(xt_v[...], lead).astype(BF)
-    rest = mm(xt_v[...], rest) + mm(gt_v[...], ctx_v[t])
-    whole[t, :, half:] = rest.astype(BF)
-    qsum_v[t] = mm(jnp.ones((8, d.shape[0]), BF), d)
-
-
-def end_rows(r, block, gh1_v, dqkv_v, a_v, gx_v):
-    rows = pl.ds(pl.multiple_of(r * block, block), block)
-    total = gh1_v[r]
-    for t in range(dqkv_v.shape[0]):
-        total = total + mm(dqkv_v[t, rows, :], a_v[t], NT)
-    gx_v[r] = total.astype(BF)
+    )(qkv, ctx, dctx, lse, seg, x, gh1, g)
 
 
 def end_vectors(sums, qsum_v, tab_v):
@@ -1021,7 +1055,7 @@
     copies = Copies(send, recv, loc)
     third = own.shape[0] // 3
     parts = []
-    for i, order in enumerate((P_Y, P_Z, P_X)):
+    for i, order in enumerate((Q_X, Q_Y, Q_Z)):
         rows = pl.ds(i * third, third)
         parts.append(ReducePart(place, copies, da, total, (r0, r1, r2, r3, r4), own, order[::-1], rows))
     rows = pl.ds(0, vec_own.shape[0])
@@ -1033,23 +1067,6 @@
         for part in parts:
             part.advance()
     wait_all(moved)
-
-
-def end_scratch(x, ctx, dqkv, width):
-    groups, length, _ = dqkv.shape
-    return [
-        pltpu.VMEM((groups, width, width), BF),
-        pltpu.VMEM(x.shape, BF),
-        pltpu.VMEM(ctx.shape, BF),
-        pltpu.VMEM(x.shape, F32),
-        pltpu.VMEM(dqkv.shape, BF),
-        pltpu.VMEM((width, length), BF),
-        pltpu.VMEM((width, length), BF),
-        pltpu.VMEM((2,) * 5 + (width // 8, width), BF),
-        pltpu.VMEM((groups, 8, width), F32),
-        pltpu.VMEM(x.shape, BF),
-        pltpu.VMEM((LANES, width), F32),
-    ]
 
 
 def sum_comm(da, vt, gx):
@@ -1077,47 +1094,20 @@
     )(da, vt, gx)
 
 
-def end_plain_kernel(g, x, ctx, gh1, dqkv, sums, da, vt, gx, a_v, x_v, ctx_v, gh1_v, dqkv_v, xt_v, gt_v, da_v, qsum_v, gx_v, tab_v, load_sem, out_sem):
-    loads = end_loads(g, x, ctx, gh1, dqkv, (a_v, x_v, ctx_v, gh1_v, dqkv_v), load_sem)
-    for load in loads:
-        load.wait()
-    end_turn(x_v, gh1_v, xt_v, gt_v)
-
-    def group(t, carry):
-        end_group(t, xt_v, gt_v, ctx_v, dqkv_v, da_v, qsum_v)
-        return carry
-
-    lax.fori_loop(0, dqkv_v.shape[0], group, 0)
-    block = gx_v.shape[1]
-
-    def rows(r, carry):
-        end_rows(r, block, gh1_v, dqkv_v, a_v, gx_v)
-        return carry
-
-    lax.fori_loop(0, gx_v.shape[0], rows, 0)
-    vt[...] = end_vectors(sums, qsum_v, tab_v)
-    copies = [pltpu.make_async_copy(da_v, da, out_sem.at[0]), pltpu.make_async_copy(gx_v, gx, out_sem.at[1])]
-    for copy in copies:
-        copy.start()
-    for copy in copies:
-        copy.wait()
-
-
-def end_plain(g, x, ctx, gh1, dqkv, sums):
-    width = x.shape[2]
+def vector_kernel(sums, qsum, vt, tab_v):
+    vt[...] = end_vectors(sums, qsum, tab_v)
+
+
+def vector_table(sums, qsum):
+    width = sums.shape[2]
     return pl.pallas_call(
-        end_plain_kernel,
-        in_specs=[ANY] * 5 + [VMEM],
-        out_specs=[ANY, VMEM, ANY],
-        out_shape=[
-            jax.ShapeDtypeStruct((2,) * 5 + (width // 8, width), BF),
-            jax.ShapeDtypeStruct((width, LANES), F32),
-            jax.ShapeDtypeStruct(x.shape, BF),
-        ],
-        scratch_shapes=end_scratch(x, ctx, dqkv, width) + [pltpu.SemaphoreType.DMA((5,)), pltpu.SemaphoreType.DMA((2,))],
-        compiler_params=params(),
-        name="weight_gradients",
-    )(g, x, ctx, gh1, dqkv, sums)
+        vector_kernel,
+        in_specs=[VMEM] * 2,
+        out_specs=VMEM,
+        out_shape=jax.ShapeDtypeStruct((width, LANES), F32),
+        scratch_shapes=[pltpu.VMEM((LANES, width), F32)],
+        name="vector_table",
+    )(sums, qsum)
 
 
 def pack(qkv_weight, out_weight, in_weight, down_weight):
@@ -1163,12 +1153,12 @@
     out, grad, gh1, dctx, sums = middle(g, x, cot, ctx, rows)
     if kernels:
         grad = grad.reshape((2,) + bits + (n, width))
-        dqkv, own, out_rows = bwd_comm(qkv, ctx, dctx, lse, seg, grad, out)
-        da, vt, gx = end_plain(g, x, ctx, gh1, dqkv, sums)
-        own_a, own_v, gx_rows = sum_comm(da, vt.reshape(bits + (fine, LANES)), gx)
+        da, gx, qsum, own, out_rows = bwd_comm(qkv, ctx, dctx, lse, seg, x, gh1, g, grad, out)
+        vt = vector_table(sums, qsum).reshape(bits + (fine, LANES))
+        own_a, own_v, gx_rows = sum_comm(da.reshape(bits + (n, width)), vt, gx)
     else:
-        dqkv = bwd_plain(qkv, ctx, dctx, lse, seg)
-        da, vt, gx = end_plain(g, x, ctx, gh1, dqkv, sums)
+        da, gx, qsum = bwd_plain(qkv, ctx, dctx, lse, seg, x, gh1, g)
+        vt = vector_table(sums, qsum)
         every_grad = jnp.concatenate([da.reshape(1, n_t, n_dp, n, width), grad.reshape(2, n_t, n_dp, n, width)])
         every_grad = every_grad.transpose(2, 1, 0, 3, 4).reshape(n_dp * n_t, 3, n, width)
         own = lax.psum_scatter(every_grad, ALL, scatter_dimension=0, tiled=True)[0].astype(F32)

time: 342 us -> 316 us (0.924)
  Pallas kernels: 324 us -> 299 us
    pallas_call x1, Pallas kernels: 27.3 us -> 2.36 us  [vector_table(): pl.pallas_call(vector_kernel, in_specs=[VMEM] * 2, out_specs=VMEM, out_sh...]
    pallas_call x1, Pallas kernels: 77 us -> 85.5 us  [bwd_comm(): pl.pallas_call(bwd_comm_kernel, in_specs=[ANY] * 3 + [VMEM] * 2 + [ANY] *...]
    pallas_call x1, Pallas kernels: 46 us -> 40.7 us  [sum_comm(): pl.pallas_call(sum_comm_kernel, in_specs=[ANY] * 3, out_specs=[VMEM, VMEM...]
    pallas_call x1, Pallas kernels: 112 us -> 108 us  [fwd_comm(): pl.pallas_call(fwd_comm_kernel, in_specs=[ANY] * 4 + [VMEM], out_specs=[A...]
    unnamed x16 -> x14, local copies, waits for them, and re-layouts: 6.92 us -> 6.92 us
where the time goes in v1:
time: 316 us
  Pallas kernels  299 us (95%)
  local copies, waits for them, and re-layouts  13.2 us (4%)
    pallas_call x1, Pallas kernels, fwd_comm(): pl.pallas_call(fwd_comm_kernel, in_specs=[ANY] * 4 + [VMEM], out_specs=[A...  108 us
    pallas_call x1, Pallas kernels, bwd_comm(): pl.pallas_call(bwd_comm_kernel, in_specs=[ANY] * 3 + [VMEM] * 2 + [ANY] *...  85.5 us
    pallas_call x1, Pallas kernels, middle(): pl.pallas_call(mid_kernel, in_specs=[ANY] * 4 + [VMEM], out_specs=[ANY] *...  62.1 us
    pallas_call x1, Pallas kernels, sum_comm(): pl.pallas_call(sum_comm_kernel, in_specs=[ANY] * 3, out_specs=[VMEM, VMEM...  40.7 us
    unnamed x14, local copies, waits for them, and re-layouts  6.92 us

profile of v1, /device:TPU:0, one launch (start us, length us, event | category | flops | bytes accessed | tf_op | source)
XLA Modules:
  0.0 315.7 jit_solution(4133131590710533024)
XLA Ops:
  0.7 0.7 copy-done
  1.4 0.8 copy.20
  2.1 0.6 pad.4.vec
  2.7 0.9 copy.19
  3.7 0.9 slice_bitcast_fusion.2
  4.7 0.1 concatenate.18
  4.8 1.8 pad_maximum_fusion.shard
  6.6 1.0 copy.21.seg
  7.6 108.3 %attention_forward.1 = (bf16[3,2,2,2,2,2,96,768]{7,6,5,4,3,2,1,0:T(8,128)(2,1)}, bf16[4,256,768]{2,1,0:T(8,128)(2,1)}, bf16[4,256,768]{2,1,0:T(8,128)(2,1)}, bf1...) custom-call(bf16[3,96,768]{2,1,0:T(8,128)(2,1)} %pad_maximum_fusion.shard, ...), custom_call_target="tpu_custom_call" | custom-call | tf_op jit(solution)/shard_map/attention_forward/pallas_call | solution.py:693
  115.9 62.1 %feed_forward.1 = (bf16[4,256,768]{2,1,0:T(8,128)(2,1)}, bf16[2,4,768,768]{3,2,1,0:T(8,128)(2,1)}, f32[4,256,768]{2,1,0:T(8,128)}, bf16[4,1024,384]{2,1,0:T(8,128)(2,1)}, f32[12,8,768]{2,1,0:T(8,128)}) custom-call(bf16[3,4,768,768]{3,2,1,0:T(8,128)(2,1)} %bitcast.35, bf16[4,256,768]{2,1,0:T(8,128)(2,1)} %get-tuple-element.30.x, ...), custom_call_target="tpu_custom_call" | custom-call | tf_op jit(solution)/shard_map/feed_forward/pallas_call | solution.py:792
  178.0 85.5 %attention_backward.1 = (bf16[4,768,768]{2,1,0:T(8,128)(2,1)}, bf16[4,256,768]{2,1,0:T(8,128)(2,1)}, f32[4,8,768]{2,1,0:T(8,128)}, f32[2,96,768]{2,1,0:T(8,128)}, bf16[4,256,768]{2,1,0:T(8,128)(2,1)}) custom-call(bf16[4,1024,768]{2,1,0:T(8,128)(2,1)} %get-tuple-element.27.qkv, bf16[4,1024,384]{2,1,0:T(8,128)(2,1)} %get-tuple-element.28.ctx, ...), custom_call_target="tpu_custom_call" | custom-call | tf_op jit(solution)/shard_map/attention_backward/pallas_call | solution.py:993
  263.6 2.4 vector_table.1
  265.9 40.7 %weight_sums.1 = (f32[96,768]{1,0:T(8,128)}, f32[24,128]{1,0:T(8,128)}, bf16[4,256,768]{2,1,0:T(8,128)(2,1)}) custom-call(bf16[2,2,2,2,2,96,768]{6,5,4,3,2,1,0:T(8,128)(2,1)} %bitcast.38, f32[2,2,2,2,2,24,128]{6,5,4,3,2,1,0:T(8,128)} %bitcast.39, bf16[4,256,768]{2,1,0:T(8,128)(2,1)} %get-tuple-element.42.gx), custom_call_target="tpu_custom_call" | custom-call | tf_op jit(solution)/shard_map/weight_sums/pallas_call | solution.py:1075
  306.6 0.8 slice_bitcast_fusion.5
  307.4 0.7 copy.24
  308.1 0.9 fusion.1
  308.9 1.1 fusion
  310.1 0.1 maximum_bitcast_fusion.3
  310.2 0.7 copy.23
  310.9 0.7 pad_maximum_fusion.1
  311.7 0.8 slice_bitcast_fusion
  312.5 1.1 copy.27
  313.7 0.8 copy-done.2
  314.5 1.1 copy.28
  (16 shorter events, 0.2 us)
Async XLA Ops:
  0.6 0.7 copy-start
  306.6 5.1 %copy-start.3 = (f32[2,96,768]{2,1,0:T(8,128)S(1)}, f32[2,96,768]{2,1,0:T(8,128)}, u32[]{:S(2)}) copy-start(f32[2,96,768]{2,1,0:T(8,128)} %get-tuple-element.45) | copy-start | bytes 1769476
  308.9 3.6 %copy-start.1 = (bf16[4,256,768]{2,1,0:T(8,128)(2,1)S(1)}, bf16[4,256,768]{2,1,0:T(8,128)(2,1)}, u32[]{:S(2)}) copy-start(bf16[4,256,768]{2,1,0:T(8,128)(2,1)} %get-tuple-element.87) | copy-start | bytes 4718596
  312.5 2.0 copy-start.2

commit v2 on v1

--- a/solution.py
+++ b/solution.py
@@ -244,7 +244,7 @@
     return x * cdf, cdf + x * tail * 0.3989422804014327
 
 
-def mid_rows(i, block, refs):
+def mid_rows(i, block, refs, late):
     (x_v, cot_v, ctx_v, ao_v, in_v, dn_v, vec, act_v, dact_v, dpre_v, y1_v, g2_v, out_v, gh1_v, dctx_v, sums_v) = refs
     rows = pl.ds(pl.multiple_of(i * block, block), block)
     groups = in_v.shape[0]
@@ -263,6 +263,7 @@
     y1_low = y1.astype(BF)
     y1_v[rows, :] = y1_low
     ffn = row(5) + y1
+    pl.when(i == 0)(lambda: wait_all(late))
     for t in range(groups):
         pre = mm(y1_low, in_v[t]) + row(8 + t)
         act, slope = gelu_both(pre)
@@ -301,8 +302,8 @@
 P_Z = ("z2", "x", "y", "z1")
 Q_Y = ("z2", "x", "z1", "y")
 Q_Z = ("z2", "x", "y", "z1")
+P_X = ("z2", "y", "z1", "x")
 Q_X = ("x", "z2", "z1", "y")
-Q_M = ("y", "z2", "x", "z1")
 
 
 class Place:
@@ -445,7 +446,8 @@
 
 
 class ReducePart:
-    def __init__(self, place, copies, src, total, arrive, out, order, rows, dims=BLOCKS):
+    def __init__(self, place, copies, src, total, arrive, out, order, rows, dims=BLOCKS, paired=False):
+        self.paired = paired
         self.place, self.copies, self.src, self.total, self.arrive = place, copies, src, total, arrive
         self.out, self.order, self.rows, self.dims = out, order, rows, dims
         self.inner = tuple(dim for dim in dims if dim != "c")
@@ -473,6 +475,9 @@
 
     def begin(self):
         p, first = self.place, self.order[0]
+        if self.paired:
+            self.keep = self.copies.here(lambda: (self.src.at[(ALLBITS,) * 4 + (self.rows,)], self.total.at[(ALLBITS,) * 4 + (self.rows,)]))
+            return
         self.side = [self.half(lambda: p.flip(first)), self.half(lambda: p.bit[first])]
         if self.kept is self.inner:
             free = {dim: ALLBITS for dim in self.inner}
@@ -512,11 +517,16 @@
         if s == 0:
             if self.kept is self.inner:
                 self.keep()
-            self.side[0]()
+            if not self.paired:
+                self.side[0]()
         else:
             self.current()
         if s < len(self.order):
             dim = self.order[s]
+            if s == 0 and self.paired:
+                self.current = self.send()
+                self.stage = 1
+                return
             self.add(dim, p.flip(dim))
             self.current = self.send()
             if s == 0:
@@ -562,8 +572,8 @@
     return [pltpu.SemaphoreType.DMA((count,))] * 2
 
 
-def fwd_core(group_ref, x_v, vt_v, seg, qkv, ctx, lse, vec_rows, s, ticks):
-    (a_v, bias_v, oh_v, km_v, qkv_v, ka_v, va_v, ctx_v, a_sem, out_sem) = s
+def fwd_core(group_ref, x_v, vt_v, seg, qkv, ctx, xt, lse, vec_rows, s, ticks):
+    (a_v, bias_v, oh_v, km_v, qkv_v, ka_v, va_v, ctx_v, xt_v, a_sem, out_sem) = s
     groups, length = qkv.shape[:2]
     block = 256
     blocks = length // block
@@ -600,6 +610,10 @@
         return carry
 
     lax.fori_loop(0, groups * blocks, step, 0)
+    xt_v[...] = flat(x_v[...]).T
+    turned = pltpu.make_async_copy(xt_v, xt, a_sem.at[0])
+    turned.start()
+    turned.wait()
     for t in range(groups):
         pltpu.make_async_copy(qkv_v.at[t], qkv.at[t], out_sem.at[0, t]).wait()
         pltpu.make_async_copy(ctx_v.at[t], ctx.at[t], out_sem.at[1, t]).wait()
@@ -615,6 +629,7 @@
         pltpu.VMEM((3, length, LANES), BF),
         pltpu.VMEM((3, length, LANES), BF),
         pltpu.VMEM((groups, length, 3 * LANES), BF),
+        pltpu.VMEM((width, length), BF),
         pltpu.SemaphoreType.DMA((2,)),
         pltpu.SemaphoreType.DMA((2, groups)),
     ]
@@ -624,62 +639,51 @@
     return [
         jax.ShapeDtypeStruct((groups, length, width), BF),
         jax.ShapeDtypeStruct((groups, length, 3 * LANES), BF),
+        jax.ShapeDtypeStruct((width, length), BF),
         jax.ShapeDtypeStruct((length, LANES), F32),
         jax.ShapeDtypeStruct((16, width), F32),
     ]
 
 
-def fwd_comm_kernel(shard, vec, tok, cot, seg, g, x, co, qkv, ctx, lse, vec_rows, x_v, vt_v, send, recv, loc, *s):
+def fwd_comm_kernel(shard, vec, tok, cot, seg, g, x, co, qkv, ctx, xt, lse, vec_rows, x_v, vt_v, send, recv, loc, *s):
     place = Place()
     enter(place)
     copies = Copies(send, recv, loc)
     mk = functools.partial(GatherPart, place, copies)
     n = shard.shape[1]
     third, half = n // 3, n // 2
-    first = [
-        mk(shard.at[0], g.at[0], Q_X, pl.ds(0, third)),
-        mk(shard.at[0], g.at[0], Q_Y, pl.ds(third, third)),
-        mk(shard.at[0], g.at[0], Q_Z, pl.ds(2 * third, third)),
-        mk(vec, vt_v, Q_Y, pl.ds(0, vec.shape[0]), FEATURES),
-    ]
-    later = [
-        mk(shard.at[1], g.at[1], Q_Y, pl.ds(0, half)),
-        mk(shard.at[1], g.at[1], Q_Z, pl.ds(half, half)),
-        mk(shard.at[2], g.at[2], Q_M, pl.ds(0, half)),
-        mk(shard.at[2], g.at[2], Q_Y, pl.ds(half, half)),
-    ]
+    first = [mk(vec, vt_v, Q_Z, pl.ds(0, vec.shape[0]), FEATURES)]
+    first += [mk(shard.at[0], g.at[0], order, pl.ds(i * third, third)) for i, order in enumerate((Q_Y, Q_Z, P_X))]
+    later = [mk(shard.at[1], g.at[1], order, pl.ds(i * half, half)) for i, order in enumerate((Q_Y, Q_Z))]
+    later += [mk(shard.at[2], g.at[2], order, pl.ds(i * third, third)) for i, order in enumerate((Q_Y, Q_Z, P_X))]
     moved = []
 
-    def advance(*which):
-        for i in which:
-            later[i].advance()
+    def advance():
+        for part in later:
+            part.advance()
 
     def cot_rows():
+        advance()
         moved.extend(start_rows(place, copies, cot, co))
 
     for part in first:
         part.begin()
-    rows = start_rows(place, copies, tok, x_v)
+    rows = [start_row(place, copies, tok, x_v, k) for k in (2, 1)] + [keep_row(place, copies, tok, x_v)]
     for stage in range(4):
         for part in first:
             part.advance()
-        if stage == 1:
+        if stage == 0:
+            rows.append(start_row(place, copies, tok, x_v, 3))
+        if stage == 2:
             for part in later:
                 part.begin()
-        if stage > 1:
-            advance(0, 1, 2, 3)
     for part in first:
         part.finish()
     wait_all(rows)
     keep = copies.here(lambda: (x_v, x))
-    ticks = [
-        (0, cot_rows),
-        (4, functools.partial(advance, 1)),
-        (7, functools.partial(advance, 0, 2, 3)),
-        (15, functools.partial(advance, 1)),
-    ]
-    fwd_core(lambda t: g.at[0, t // 2, t % 2], x_v, vt_v, seg, qkv, ctx, lse, vec_rows, s, ticks)
-    advance(2, 0, 3)
+    ticks = [(1, cot_rows), (4, advance), (8, advance)]
+    fwd_core(lambda t: g.at[0, t // 2, t % 2], x_v, vt_v, seg, qkv, ctx, xt, lse, vec_rows, s, ticks)
+    advance()
     for part in later:
         part.finish()
     wait_all(moved)
@@ -693,7 +697,7 @@
     return pl.pallas_call(
         fwd_comm_kernel,
         in_specs=[ANY] * 4 + [VMEM],
-        out_specs=[ANY] * 5 + [VMEM] * 2,
+        out_specs=[ANY] * 6 + [VMEM] * 2,
         out_shape=[
             jax.ShapeDtypeStruct((3,) + bits + shard.shape[1:], BF),
             jax.ShapeDtypeStruct(tok.shape, BF),
@@ -703,7 +707,7 @@
         scratch_shapes=[
             pltpu.VMEM(tok.shape, BF),
             pltpu.VMEM(bits + vec.shape, F32),
-            *sems(80),
+            *sems(96),
             pltpu.SemaphoreType.DMA((20,)),
         ]
         + fwd_scratch(groups, length, width),
@@ -712,11 +716,11 @@
     )(shard, vec, tok, cot, seg)
 
 
-def fwd_plain_kernel(g, x, vt, seg, qkv, ctx, lse, vec_rows, sem, x_v, *s):
+def fwd_plain_kernel(g, x, vt, seg, qkv, ctx, xt, lse, vec_rows, sem, x_v, *s):
     copy = pltpu.make_async_copy(x, x_v, sem)
     copy.start()
     copy.wait()
-    fwd_core(lambda t: g.at[0, t // 2, t % 2], x_v, vt, seg, qkv, ctx, lse, vec_rows, s, [])
+    fwd_core(lambda t: g.at[0, t // 2, t % 2], x_v, vt, seg, qkv, ctx, xt, lse, vec_rows, s, [])
 
 
 def fwd_plain(g, x, vt, seg):
@@ -725,7 +729,7 @@
     return pl.pallas_call(
         fwd_plain_kernel,
         in_specs=[ANY, ANY, VMEM, VMEM],
-        out_specs=[ANY] * 2 + [VMEM] * 2,
+        out_specs=[ANY] * 3 + [VMEM] * 2,
         out_shape=fwd_shapes(groups, length, width),
         scratch_shapes=[pltpu.SemaphoreType.DMA, pltpu.VMEM(x.shape, BF)] + fwd_scratch(groups, length, width),
         compiler_params=params(),
@@ -747,12 +751,12 @@
     for load in loads:
         load.start()
     sums[...] = jnp.zeros_like(sums)
-    for load in loads:
+    for load in loads[:3]:
         load.wait()
     refs = (x_v, cot_v, ctx_v, ao_v, in_v, dn_v, vec, act_v, dact_v, dpre_v, y1_v, g2_v, out_v, gh1_v, dctx_v, sums)
 
     def step(i, carry):
-        mid_rows(i, block, refs)
+        mid_rows(i, block, refs, [load.wait for load in loads[3:]])
         pltpu.make_async_copy(out_v.at[i], out.at[i], out_sem.at[0, i]).start()
         pltpu.make_async_copy(gh1_v.at[i], gh1.at[i], out_sem.at[1, i]).start()
         return carry
@@ -824,15 +828,23 @@
     )(g, x, cot, ctx, vec)
 
 
-def bwd_core(qkv, ctx, dctx, lse, seg, x, gh1, g, da, gx, qsum, s, ticks):
-    (qkv_v, ctx_v, dctx_v, a_v, oh_v, km_v, qa_v, ka_v, va_v, da_v, kt_v, dqt_v, dqkv_v, x_v, gx_v, xt_v, gt_v, dw_v, in_sem, out_sem, x_sem) = s
+def bwd_core(qkv, ctx, dctx, lse, seg, xt, gh1, g, da, gx, qsum, s, ticks, place=None):
+    (qkv_v, ctx_v, dctx_v, a_v, oh_v, km_v, qa_v, ka_v, va_v, da_v, kt_v, dqt_v, dqkv_v, x_v, gx_v, xt_v, gt_v, dw_v, pair_v, in_sem, out_sem, x_sem, pair_sem) = s
     groups, length = qkv.shape[:2]
     block = 256
     blocks = length // block
     half = 3 * LANES
 
-    def loads(t):
-        slot = t % 2
+    early = groups if place is None else groups // 2
+
+    def group(i):
+        if place is None:
+            return i
+        core = place.bit["c"]
+        return 2 * (i % 2) + core + (1 - i // 2) * (1 - 2 * core)
+
+    def loads(i):
+        t, slot = group(i), i % 2
         return [
             pltpu.make_async_copy(qkv.at[t], qkv_v.at[slot], in_sem.at[0, slot]),
             pltpu.make_async_copy(ctx.at[t], ctx_v.at[slot], in_sem.at[1, slot]),
@@ -840,49 +852,67 @@
             pltpu.make_async_copy(g.at[0, t], a_v.at[slot], in_sem.at[3, slot]),
         ]
 
-    def result(t):
-        return pltpu.make_async_copy(dw_v.at[t], da.at[t], out_sem.at[t])
-
-    more = [pltpu.make_async_copy(x, x_v, x_sem.at[0]), pltpu.make_async_copy(gh1, gx_v, x_sem.at[1])]
+    def result(i):
+        if place is None:
+            return pltpu.make_async_copy(dw_v.at[i], da.at[i], out_sem.at[i])
+        return pltpu.make_async_copy(dw_v.at[i], da.at[i - early], out_sem.at[i])
+
+    def hand_over(i):
+        return pltpu.make_async_remote_copy(
+            src_ref=dw_v.at[i],
+            dst_ref=pair_v.at[i],
+            send_sem=pair_sem.at[0, i],
+            recv_sem=pair_sem.at[1, i],
+            device_id=place.peer("c"),
+            device_id_type=MESH,
+        )
+
+    more = [pltpu.make_async_copy(xt, xt_v, x_sem.at[0]), pltpu.make_async_copy(gh1, gx_v, x_sem.at[1])]
     for load in loads(0) + more:
         load.start()
     oh_v[...] = jnp.where(seg[...] == lane_ids(oh_v.shape) % HD, 1.0, 0.0).astype(BF)
     km_v[...] = key_marks(seg, km_v.shape)
-    for load in more:
-        load.wait()
-    xt_v[...] = flat(x_v[...]).T
-    gt_v[...] = flat(gx_v[...]).astype(BF).T
-
-    def weights(t, slot):
+
+    def ready():
+        for load in more:
+            load.wait()
+        gt_v[...] = flat(gx_v[...]).astype(BF).T
+
+    def weights(i, slot, add):
         def chunk(r, inner):
             part = pl.ds(pl.multiple_of(r * block, block), block)
-            dw_v[t, part, :half] = mm(xt_v[part, :], dqkv_v[:, :half]).astype(BF)
-            dw_v[t, part, half:] = (mm(xt_v[part, :], dqkv_v[:, half:]) + mm(gt_v[part, :], ctx_v[slot])).astype(BF)
+            lead = mm(xt_v[part, :], dqkv_v[:, :half])
+            rest = mm(xt_v[part, :], dqkv_v[:, half:]) + mm(gt_v[part, :], ctx_v[slot])
+            if add:
+                lead = lead + pair_v[i - early, part, :half].astype(F32)
+                rest = rest + pair_v[i - early, part, half:].astype(F32)
+            dw_v[i, part, :half] = lead.astype(BF)
+            dw_v[i, part, half:] = rest.astype(BF)
             return inner
 
         lax.fori_loop(0, dw_v.shape[1] // block, chunk, 0)
-        qsum[t] = mm(jnp.ones((8, length), BF), dqkv_v[...])
 
     def rows(b, slot):
         part = pl.ds(pl.multiple_of(b * block, block), block)
         gx_v[b] = gx_v[b] + mm(dqkv_v[part, :], a_v[slot], NT)
 
     def step(i, carry):
-        t, b = i // blocks, i % blocks
-        slot = t % 2
+        at, b = i // blocks, i % blocks
+        slot = at % 2
         at_tick(i, ticks)
+        pl.when(i == 1)(ready)
 
         @pl.when(b == 0)
         def _():
-            for load in loads(t):
+            for load in loads(at):
                 load.wait()
 
-            @pl.when(t + 1 < groups)
+            @pl.when(at + 1 < groups)
             def _():
-                for load in loads(t + 1):
+                for load in loads(at + 1):
                     load.start()
 
-            bwd_group(t, qkv_v.at[slot], ctx_v.at[slot], dctx_v.at[slot], lse, oh_v, km_v, qa_v, ka_v, va_v, da_v, kt_v, dqt_v)
+            bwd_group(group(at), qkv_v.at[slot], ctx_v.at[slot], dctx_v.at[slot], lse, oh_v, km_v, qa_v, ka_v, va_v, da_v, kt_v, dqt_v)
 
         part = pl.ds(pl.multiple_of(b * block, block), block)
         bwd_block(part, block, qa_v, ka_v, va_v, da_v, kt_v, dqt_v, dqkv_v)
@@ -890,8 +920,22 @@
         @pl.when(b == blocks - 1)
         def _():
             bwd_finish(dqt_v, dqkv_v)
-            weights(t, slot)
-            result(t).start()
+            qsum[group(at)] = mm(jnp.ones((8, length), BF), dqkv_v[...])
+            if place is None:
+                weights(at, slot, False)
+                result(at).start()
+            else:
+
+                @pl.when(at < early)
+                def _():
+                    weights(at, slot, False)
+                    hand_over(at).start()
+
+                @pl.when(at >= early)
+                def _():
+                    hand_over(at - early).wait()
+                    weights(at, slot, True)
+                    result(at).start()
 
             def row_step(r, inner):
                 rows(r, slot)
@@ -910,8 +954,8 @@
     lax.fori_loop(0, blocks, low_step, 0)
     last = pltpu.make_async_copy(x_v, gx, x_sem.at[0])
     last.start()
-    for t in range(groups):
-        result(t).wait()
+    for i in range(0 if place is None else early, groups):
+        result(i).wait()
     last.wait()
 
 
@@ -936,21 +980,23 @@
         pltpu.VMEM((width, length), BF),
         pltpu.VMEM((width, length), BF),
         pltpu.VMEM((groups, width, width), BF),
+        pltpu.VMEM((groups // 2, width, width), BF),
         pltpu.SemaphoreType.DMA((4, 2)),
         pltpu.SemaphoreType.DMA((groups,)),
         pltpu.SemaphoreType.DMA((2,)),
+        pltpu.SemaphoreType.DMA((2, groups // 2)),
     ]
 
 
-def bwd_shapes(groups, width, x):
+def bwd_shapes(groups, width, x, held):
     return [
-        jax.ShapeDtypeStruct((groups, width, width), BF),
+        jax.ShapeDtypeStruct((held, width, width), BF),
         jax.ShapeDtypeStruct(x, BF),
         jax.ShapeDtypeStruct((groups, 8, width), F32),
     ]
 
 
-def bwd_comm_kernel(qkv, ctx, dctx, lse, seg, x, gh1, g, grad, out, da, gx, qsum, own, out_rows, total, r0, r1, r2, r3, r4, r5, r6, r7, r8, r9, send, recv, loc, *s):
+def bwd_comm_kernel(qkv, ctx, dctx, lse, seg, xt, gh1, g, grad, out, da, gx, qsum, own, out_rows, total, r0, r1, r2, r3, r4, r5, r6, r7, r8, r9, send, recv, loc, *s):
     place = Place()
     enter(place)
     copies = Copies(send, recv, loc)
@@ -981,12 +1027,12 @@
         (14, functools.partial(advance, 0, 2)),
         (15, functools.partial(advance, 1, 3)),
     ]
-    bwd_core(qkv, ctx, dctx, lse, seg, x, gh1, g, da, gx, qsum, s, ticks)
+    bwd_core(qkv, ctx, dctx, lse, seg, xt, gh1, g, da, gx, qsum, s, ticks, place)
     advance(0, 1, 2, 3)
     wait_all(moved)
 
 
-def bwd_comm(qkv, ctx, dctx, lse, seg, x, gh1, g, grad, out):
+def bwd_comm(qkv, ctx, dctx, lse, seg, xt, gh1, g, grad, out):
     groups, length, width = qkv.shape
     n = grad.shape[6]
     arrive = arrivals(n, width, BF)
@@ -994,7 +1040,7 @@
         bwd_comm_kernel,
         in_specs=[ANY] * 3 + [VMEM] * 2 + [ANY] * 5,
         out_specs=[ANY, ANY, VMEM, VMEM, ANY],
-        out_shape=bwd_shapes(groups, width, x.shape)
+        out_shape=bwd_shapes(groups, width, gh1.shape, groups // 2)
         + [
             jax.ShapeDtypeStruct((2, n, width), F32),
             jax.ShapeDtypeStruct(out.shape, BF),
@@ -1006,27 +1052,27 @@
             *sems(40),
             pltpu.SemaphoreType.DMA((10,)),
         ]
-        + bwd_scratch(groups, length, width, x.shape),
+        + bwd_scratch(groups, length, width, gh1.shape),
         compiler_params=params(1),
         name="attention_backward",
-    )(qkv, ctx, dctx, lse, seg, x, gh1, g, grad, out)
-
-
-def bwd_plain_kernel(qkv, ctx, dctx, lse, seg, x, gh1, g, da, gx, qsum, *s):
-    bwd_core(qkv, ctx, dctx, lse, seg, x, gh1, g, da, gx, qsum, s, [])
-
-
-def bwd_plain(qkv, ctx, dctx, lse, seg, x, gh1, g):
+    )(qkv, ctx, dctx, lse, seg, xt, gh1, g, grad, out)
+
+
+def bwd_plain_kernel(qkv, ctx, dctx, lse, seg, xt, gh1, g, da, gx, qsum, *s):
+    bwd_core(qkv, ctx, dctx, lse, seg, xt, gh1, g, da, gx, qsum, s, [])
+
+
+def bwd_plain(qkv, ctx, dctx, lse, seg, xt, gh1, g):
     groups, length, width = qkv.shape
     return pl.pallas_call(
         bwd_plain_kernel,
         in_specs=[ANY] * 3 + [VMEM] * 2 + [ANY] * 3,
         out_specs=[ANY, ANY, VMEM],
-        out_shape=bwd_shapes(groups, width, x.shape),
-        scratch_shapes=bwd_scratch(groups, length, width, x.shape),
+        out_shape=bwd_shapes(groups, width, gh1.shape, groups),
+        scratch_shapes=bwd_scratch(groups, length, width, gh1.shape),
         compiler_params=params(),
         name="attention_backward",
-    )(qkv, ctx, dctx, lse, seg, x, gh1, g)
+    )(qkv, ctx, dctx, lse, seg, xt, gh1, g)
 
 
 def end_vectors(sums, qsum_v, tab_v):
@@ -1049,7 +1095,7 @@
     return table
 
 
-def sum_comm_kernel(da, vt, gx, own, vec_own, gx_rows, total, vtot, r0, r1, r2, r3, r4, r5, r6, r7, r8, r9, send, recv, loc):
+def sum_comm_kernel(da, vt, gx, own, vec_own, gx_rows, total, vtot, r0, r1, r2, r3, r4, r5, r6, r7, r8, send, recv, loc):
     place = Place()
     enter(place)
     copies = Copies(send, recv, loc)
@@ -1057,9 +1103,9 @@
     parts = []
     for i, order in enumerate((Q_X, Q_Y, Q_Z)):
         rows = pl.ds(i * third, third)
-        parts.append(ReducePart(place, copies, da, total, (r0, r1, r2, r3, r4), own, order[::-1], rows))
+        parts.append(ReducePart(place, copies, da, total, (r0, r0, r1, r2, r3), own, order[::-1], rows, paired=True))
     rows = pl.ds(0, vec_own.shape[0])
-    parts.append(ReducePart(place, copies, vt, vtot, (r5, r6, r7, r8, r9), vec_own, P_Y[::-1], rows, FEATURES))
+    parts.append(ReducePart(place, copies, vt, vtot, (r4, r5, r6, r7, r8), vec_own, P_Y[::-1], rows, FEATURES))
     for part in parts:
         part.begin()
     moved = start_rows(place, copies, gx, gx_rows)
@@ -1084,7 +1130,7 @@
         scratch_shapes=[
             pltpu.VMEM((2,) * 4 + (n, width), BF),
             pltpu.VMEM((2,) * 4 + (fine, LANES), F32),
-            *arrivals(n, width, BF),
+            *arrivals(n, width, BF)[1:],
             *arrivals(fine, LANES, F32),
             *sems(40),
             pltpu.SemaphoreType.DMA((10,)),
@@ -1141,23 +1187,23 @@
     kernels = n_dp == 8 and n_t == 4
     bits = (2,) * 5
     if kernels:
-        g, x, cot, qkv, ctx, lse, rows = fwd_comm(shard, vec, tokens, cotangent, seg)
+        g, x, cot, qkv, ctx, xt, lse, rows = fwd_comm(shard, vec, tokens, cotangent, seg)
     else:
         full = lax.all_gather(shard, ALL, axis=0, tiled=False).reshape(n_dp, n_t, 3, n, width)
         g = full.transpose(2, 1, 0, 3, 4).reshape((3,) + bits + (width // 8, width))
         vt = lax.all_gather(vec, ALL, axis=0, tiled=True)
         x = lax.all_to_all(tokens, "tensor", split_axis=0, concat_axis=0, tiled=True)
         cot = lax.all_to_all(cotangent, "tensor", split_axis=0, concat_axis=0, tiled=True)
-        qkv, ctx, lse, rows = fwd_plain(g, x, vt, seg)
+        qkv, ctx, xt, lse, rows = fwd_plain(g, x, vt, seg)
     g = g.reshape(3, groups, width, width)
     out, grad, gh1, dctx, sums = middle(g, x, cot, ctx, rows)
     if kernels:
         grad = grad.reshape((2,) + bits + (n, width))
-        da, gx, qsum, own, out_rows = bwd_comm(qkv, ctx, dctx, lse, seg, x, gh1, g, grad, out)
+        da, gx, qsum, own, out_rows = bwd_comm(qkv, ctx, dctx, lse, seg, xt, gh1, g, grad, out)
         vt = vector_table(sums, qsum).reshape(bits + (fine, LANES))
-        own_a, own_v, gx_rows = sum_comm(da.reshape(bits + (n, width)), vt, gx)
+        own_a, own_v, gx_rows = sum_comm(da.reshape(bits[1:] + (n, width)), vt, gx)
     else:
-        da, gx, qsum = bwd_plain(qkv, ctx, dctx, lse, seg, x, gh1, g)
+        da, gx, qsum = bwd_plain(qkv, ctx, dctx, lse, seg, xt, gh1, g)
         vt = vector_table(sums, qsum)
         every_grad = jnp.concatenate([da.reshape(1, n_t, n_dp, n, width), grad.reshape(2, n_t, n_dp, n, width)])
         every_grad = every_grad.transpose(2, 1, 0, 3, 4).reshape(n_dp * n_t, 3, n, width)

time: 316 us -> 308 us (0.975)
  Pallas kernels: 299 us -> 291 us
where the time goes in v2:
time: 308 us
  Pallas kernels  291 us (94%)
  local copies, waits for them, and re-layouts  13.2 us (4%)
    pallas_call x1, Pallas kernels, fwd_comm(): pl.pallas_call(fwd_comm_kernel, in_specs=[ANY] * 4 + [VMEM], out_specs=[A...  106 us
    pallas_call x1, Pallas kernels, bwd_comm(): pl.pallas_call(bwd_comm_kernel, in_specs=[ANY] * 3 + [VMEM] * 2 + [ANY] *...  83.6 us
    pallas_call x1, Pallas kernels, middle(): pl.pallas_call(mid_kernel, in_specs=[ANY] * 4 + [VMEM], out_specs=[ANY] *...  61.1 us
    pallas_call x1, Pallas kernels, sum_comm(): pl.pallas_call(sum_comm_kernel, in_specs=[ANY] * 3, out_specs=[VMEM, VMEM...  38.4 us
    unnamed x14, local copies, waits for them, and re-layouts  6.92 us

profile of v2, /device:TPU:0, one launch (start us, length us, event | category | flops | bytes accessed | tf_op | source)
XLA Modules:
  0.0 307.6 jit_solution(10742578990944693637)
XLA Ops:
  0.7 0.7 copy-done
  1.4 0.8 copy.20
  2.1 0.6 pad.4.vec
  2.7 0.9 copy.19
  3.7 0.9 slice_bitcast_fusion.2
  4.7 0.1 concatenate.18
  4.8 1.8 pad_maximum_fusion.shard
  6.6 1.0 copy.21.seg
  7.6 105.5 %attention_forward.1 = (bf16[3,2,2,2,2,2,96,768]{7,6,5,4,3,2,1,0:T(8,128)(2,1)}, bf16[4,256,768]{2,1,0:T(8,128)(2,1)}, bf16[4,256,768]{2,1,0:T(8,128)(2,1)}, bf1...) custom-call(bf16[3,96,768]{2,1,0:T(8,128)(2,1)} %pad_maximum_fusion., ...), custom_call_target="tpu_custom_call" | custom-call | tf_op jit(solution)/shard_map/attention_forward/pallas_call | solution.py:697
  113.1 61.1 %feed_forward.1 = (bf16[4,256,768]{2,1,0:T(8,128)(2,1)}, bf16[2,4,768,768]{3,2,1,0:T(8,128)(2,1)}, f32[4,256,768]{2,1,0:T(8,128)}, bf16[4,1024,384]{2,1,0:T(8,128)(2,1)}, f32[12,8,768]{2,1,0:T(8,128)}) custom-call(bf16[3,4,768,768]{3,2,1,0:T(8,128)(2,1)} %bitcast.35, bf16[4,256,768]{2,1,0:T(8,128)(2,1)} %get-tuple-element.31.x, ...), custom_call_target="tpu_custom_call" | custom-call | tf_op jit(solution)/shard_map/feed_forward/pallas_call | solution.py:796
  174.2 83.6 %attention_backward.1 = (bf16[2,768,768]{2,1,0:T(8,128)(2,1)}, bf16[4,256,768]{2,1,0:T(8,128)(2,1)}, f32[4,8,768]{2,1,0:T(8,128)}, f32[2,96,768]{2,1,0:T(8,128)}, bf16[4,256,768]{2,1,0:T(8,128)(2,1)}) custom-call(bf16[4,1024,768]{2,1,0:T(8,128)(2,1)} %get-tuple-element.28.qkv, bf16[4,1024,384]{2,1,0:T(8,128)(2,1)} %get-tuple-element.29.ctx, ...), custom_call_target="tpu_custom_call" | custom-call | tf_op jit(solution)/shard_map/attention_backward/pallas_call | solution.py:1039
  257.8 2.4 vector_table.1
  260.2 38.4 %weight_sums.1 = (f32[96,768]{1,0:T(8,128)}, f32[24,128]{1,0:T(8,128)}, bf16[4,256,768]{2,1,0:T(8,128)(2,1)}) custom-call(bf16[2,2,2,2,96,768]{5,4,3,2,1,0:T(8,128)(2,1)} %bitcast.38, f32[2,2,2,2,2,24,128]{6,5,4,3,2,1,0:T(8,128)} %bitcast.39, bf16[4,256,768]{2,1,0:T(8,128)(2,1)} %get-tuple-element.44.gx), custom_call_target="tpu_custom_call" | custom-call | tf_op jit(solution)/shard_map/weight_sums/pallas_call | solution.py:1121
  298.6 0.8 slice_bitcast_fusion.5
  299.3 0.7 copy.24
  300.0 0.9 fusion.1
  300.9 1.1 fusion
  302.0 0.1 maximum_bitcast_fusion.3
  302.1 0.7 copy.23
  302.9 0.7 pad_maximum_fusion.1
  303.7 0.8 slice_bitcast_fusion
  304.5 1.1 copy.27
  305.7 0.8 copy-done.2
  306.5 1.1 copy.28
  (16 shorter events, 0.2 us)
Async XLA Ops:
  0.6 0.7 copy-start
  298.6 5.1 %copy-start.3 = (f32[2,96,768]{2,1,0:T(8,128)S(1)}, f32[2,96,768]{2,1,0:T(8,128)}, u32[]{:S(2)}) copy-start(f32[2,96,768]{2,1,0:T(8,128)} %get-tuple-element.47) | copy-start | bytes 1769476
  300.9 3.6 %copy-start.1 = (bf16[4,256,768]{2,1,0:T(8,128)(2,1)S(1)}, bf16[4,256,768]{2,1,0:T(8,128)(2,1)}, u32[]{:S(2)}) copy-start(bf16[4,256,768]{2,1,0:T(8,128)(2,1)} %get-tuple-element.89) | copy-start | bytes 4718596
  304.5 2.0 copy-start.2

commit v3 on v2

--- a/solution.py
+++ b/solution.py
@@ -247,6 +247,9 @@
 def mid_rows(i, block, refs, late):
     (x_v, cot_v, ctx_v, ao_v, in_v, dn_v, vec, act_v, dact_v, dpre_v, y1_v, g2_v, out_v, gh1_v, dctx_v, sums_v) = refs
     rows = pl.ds(pl.multiple_of(i * block, block), block)
+    few = block // x_v.shape[1]
+    these = pl.ds(i * few, few)
+    apart = (few, *x_v.shape[1:])
     groups = in_v.shape[0]
 
     def row(k):
@@ -258,7 +261,7 @@
     attn = mm(ctx_v[0, rows, :], ao_v[0], NT)
     for t in range(1, groups):
         attn = attn + mm(ctx_v[t, rows, :], ao_v[t], NT)
-    h1 = x_v[i].astype(F32) + attn + row(4)
+    h1 = flat(x_v[these]).astype(F32) + attn + row(4)
     y1, u1, r1 = normalize(h1, row(0), row(1))
     y1_low = y1.astype(BF)
     y1_v[rows, :] = y1_low
@@ -272,8 +275,8 @@
         dact_v[t] = slope.astype(BF)
         ffn = ffn + mm(act, dn_v[t], NT)
     out, u2, r2 = normalize(ffn, row(2), row(3))
-    out_v[i] = out.astype(BF)
-    up = cot_v[i].astype(F32)
+    out_v[these] = out.astype(BF).reshape(apart)
+    up = flat(cot_v[these]).astype(F32)
     g_h2 = normalize_back(up, u2, r2, row(2))
     note(2, up * u2)
     note(3, up)
@@ -290,7 +293,7 @@
     note(1, g_y1)
     g_h1 = normalize_back(g_y1, u1, r1, row(0))
     note(4, g_h1)
-    gh1_v[i] = g_h1
+    gh1_v[these] = g_h1.reshape(apart)
     g1 = g_h1.astype(BF)
     for t in range(groups):
         dctx_v[t, rows, :] = mm(g1, ao_v[t]).astype(BF)
@@ -303,7 +306,6 @@
 Q_Y = ("z2", "x", "z1", "y")
 Q_Z = ("z2", "x", "y", "z1")
 P_X = ("z2", "y", "z1", "x")
-Q_X = ("x", "z2", "z1", "y")
 
 
 class Place:
@@ -742,6 +744,7 @@
     width = x.shape[2]
     half = width // 2
     blocks, block = x.shape[:2]
+    few = dact_v.shape[1] // block
 
     def copy(src, dst, i):
         return pltpu.make_async_copy(src, dst, sem.at[i])
@@ -756,12 +759,14 @@
     refs = (x_v, cot_v, ctx_v, ao_v, in_v, dn_v, vec, act_v, dact_v, dpre_v, y1_v, g2_v, out_v, gh1_v, dctx_v, sums)
 
     def step(i, carry):
-        mid_rows(i, block, refs, [load.wait for load in loads[3:]])
-        pltpu.make_async_copy(out_v.at[i], out.at[i], out_sem.at[0, i]).start()
-        pltpu.make_async_copy(gh1_v.at[i], gh1.at[i], out_sem.at[1, i]).start()
+        mid_rows(i, few * block, refs, [load.wait for load in loads[3:]])
+        for j in range(few):
+            b = i * few + j
+            pltpu.make_async_copy(out_v.at[b], out.at[b], out_sem.at[0, b]).start()
+            pltpu.make_async_copy(gh1_v.at[b], gh1.at[b], out_sem.at[1, b]).start()
         return carry
 
-    lax.fori_loop(0, blocks, step, 0)
+    lax.fori_loop(0, blocks // few, step, 0)
     send = copy(dctx_v, dctx, 0)
     send.start()
     t_v[...] = y1_v[...].T
@@ -1021,11 +1026,11 @@
     ticks = [
         (2, functools.partial(advance, 0, 1, 2, 3)),
         (3, rows),
-        (9, functools.partial(advance, 0, 1, 2, 3)),
-        (12, functools.partial(advance, 0, 2)),
-        (13, functools.partial(advance, 1, 3)),
-        (14, functools.partial(advance, 0, 2)),
-        (15, functools.partial(advance, 1, 3)),
+        (8, functools.partial(advance, 0, 1, 2, 3)),
+        (11, functools.partial(advance, 0, 2)),
+        (12, functools.partial(advance, 1, 3)),
+        (13, functools.partial(advance, 0, 2)),
+        (14, functools.partial(advance, 1, 3)),
     ]
     bwd_core(qkv, ctx, dctx, lse, seg, xt, gh1, g, da, gx, qsum, s, ticks, place)
     advance(0, 1, 2, 3)
@@ -1101,17 +1106,21 @@
     copies = Copies(send, recv, loc)
     third = own.shape[0] // 3
     parts = []
-    for i, order in enumerate((Q_X, Q_Y, Q_Z)):
+    for i, order in enumerate((P_X, Q_Y, Q_Z)):
         rows = pl.ds(i * third, third)
         parts.append(ReducePart(place, copies, da, total, (r0, r0, r1, r2, r3), own, order[::-1], rows, paired=True))
     rows = pl.ds(0, vec_own.shape[0])
     parts.append(ReducePart(place, copies, vt, vtot, (r4, r5, r6, r7, r8), vec_own, P_Y[::-1], rows, FEATURES))
     for part in parts:
         part.begin()
-    moved = start_rows(place, copies, gx, gx_rows)
+    moved = []
     for stage in range(5):
         for part in parts:
             part.advance()
+        if stage == 0:
+            moved += [start_row(place, copies, gx, gx_rows, k) for k in (2, 1)] + [keep_row(place, copies, gx, gx_rows)]
+        if stage == 2:
+            moved.append(start_row(place, copies, gx, gx_rows, 3))
     wait_all(moved)
 
 

time: 308 us -> 304 us (0.987)
  Pallas kernels: 291 us -> 285 us
    pallas_call x1, Pallas kernels: 38.4 us -> 34.9 us  [sum_comm(): pl.pallas_call(sum_comm_kernel, in_specs=[ANY] * 3, out_specs=[VMEM, VMEM...]
where the time goes in v3:
time: 304 us; the launch traced here: 302 us
  Pallas kernels  285 us (94%)
  local copies, waits for them, and re-layouts  13.2 us (4%)
    pallas_call x1, Pallas kernels, fwd_comm(): pl.pallas_call(fwd_comm_kernel, in_specs=[ANY] * 4 + [VMEM], out_specs=[A...  106 us
    pallas_call x1, Pallas kernels, bwd_comm(): pl.pallas_call(bwd_comm_kernel, in_specs=[ANY] * 3 + [VMEM] * 2 + [ANY] *...  81.5 us
    pallas_call x1, Pallas kernels, middle(): pl.pallas_call(mid_kernel, in_specs=[ANY] * 4 + [VMEM], out_specs=[ANY] *...  61.1 us
    pallas_call x1, Pallas kernels, sum_comm(): pl.pallas_call(sum_comm_kernel, in_specs=[ANY] * 3, out_specs=[VMEM, VMEM...  34.9 us
    unnamed x14, local copies, waits for them, and re-layouts  6.92 us

profile of v3, /device:TPU:0, one launch (start us, length us, event | category | flops | bytes accessed | tf_op | source)
XLA Modules:
  0.0 302.0 jit_solution(12568349655114202015)
XLA Ops:
  0.7 0.7 copy-done
  1.4 0.8 copy.20
  2.1 0.6 pad.4.vec
  2.7 0.9 copy.19
  3.7 0.9 slice_bitcast_fusion.2
  4.7 0.1 concatenate.18
  4.8 1.8 pad_maximum_fusion.shard
  6.6 1.0 copy.21.seg
  7.6 105.5 %attention_forward.1 = (bf16[3,2,2,2,2,2,96,768]{7,6,5,4,3,2,1,0:T(8,128)(2,1)}, bf16[4,256,768]{2,1,0:T(8,128)(2,1)}, bf16[4,256,768]{2,1,0:T(8,128)(2,1)}, bf1...) custom-call(bf16[3,96,768]{2,1,0:T(8,128)(2,1)} %pad_maximum_fusion., ...), custom_call_target="tpu_custom_call" | custom-call | tf_op jit(solution)/shard_map/attention_forward/pallas_call | solution.py:699
  113.1 61.1 %feed_forward.1 = (bf16[4,256,768]{2,1,0:T(8,128)(2,1)}, bf16[2,4,768,768]{3,2,1,0:T(8,128)(2,1)}, f32[4,256,768]{2,1,0:T(8,128)}, bf16[4,1024,384]{2,1,0:T(8,128)(2,1)}, f32[12,8,768]{2,1,0:T(8,128)}) custom-call(bf16[3,4,768,768]{3,2,1,0:T(8,128)(2,1)} %bitcast.35, bf16[4,256,768]{2,1,0:T(8,128)(2,1)} %get-tuple-element.31.x, ...), custom_call_target="tpu_custom_call" | custom-call | tf_op jit(solution)/shard_map/feed_forward/pallas_call | solution.py:801
  174.2 81.5 %attention_backward.1 = (bf16[2,768,768]{2,1,0:T(8,128)(2,1)}, bf16[4,256,768]{2,1,0:T(8,128)(2,1)}, f32[4,8,768]{2,1,0:T(8,128)}, f32[2,96,768]{2,1,0:T(8,128)}, bf16[4,256,768]{2,1,0:T(8,128)(2,1)}) custom-call(bf16[4,1024,768]{2,1,0:T(8,128)(2,1)} %get-tuple-element.28.qkv, bf16[4,1024,384]{2,1,0:T(8,128)(2,1)} %get-tuple-element.29.ctx, ...), custom_call_target="tpu_custom_call" | custom-call | tf_op jit(solution)/shard_map/attention_backward/pallas_call | solution.py:1044
  255.7 2.4 vector_table.1
  258.1 34.9 %weight_sums.1 = (f32[96,768]{1,0:T(8,128)}, f32[24,128]{1,0:T(8,128)}, bf16[4,256,768]{2,1,0:T(8,128)(2,1)}) custom-call(bf16[2,2,2,2,96,768]{5,4,3,2,1,0:T(8,128)(2,1)} %bitcast.38, f32[2,2,2,2,2,24,128]{6,5,4,3,2,1,0:T(8,128)} %bitcast.39, bf16[4,256,768]{2,1,0:T(8,128)(2,1)} %get-tuple-element.44.gx), custom_call_target="tpu_custom_call" | custom-call | tf_op jit(solution)/shard_map/weight_sums/pallas_call | solution.py:1130
  293.0 0.8 slice_bitcast_fusion.5
  293.8 0.7 copy.24
  294.4 0.9 fusion.1
  295.3 1.1 fusion
  296.4 0.1 maximum_bitcast_fusion.3
  296.5 0.7 copy.23
  297.3 0.7 pad_maximum_fusion.1
  298.1 0.8 slice_bitcast_fusion
  298.9 1.1 copy.27
  300.1 0.8 copy-done.2
  300.9 1.1 copy.28
  (16 shorter events, 0.2 us)
Async XLA Ops:
  0.6 0.7 copy-start
  293.0 5.1 %copy-start.3 = (f32[2,96,768]{2,1,0:T(8,128)S(1)}, f32[2,96,768]{2,1,0:T(8,128)}, u32[]{:S(2)}) copy-start(f32[2,96,768]{2,1,0:T(8,128)} %get-tuple-element.47) | copy-start | bytes 1769476
  295.3 3.6 %copy-start.1 = (bf16[4,256,768]{2,1,0:T(8,128)(2,1)S(1)}, bf16[4,256,768]{2,1,0:T(8,128)(2,1)}, u32[]{:S(2)}) copy-start(bf16[4,256,768]{2,1,0:T(8,128)(2,1)} %get-tuple-element.89) | copy-start | bytes 4718596
  298.9 2.0 copy-start.2

commit v4 on v3

--- a/solution.py
+++ b/solution.py
@@ -238,8 +238,8 @@
     a = jnp.abs(x)
     tail = jnp.exp2(x * x * (-0.5 * LOG2E))
     t = 1.0 / (1.0 + (0.3275911 * 0.5**0.5) * a)
-    poly = ((((1.061405429 * t - 1.453152027) * t + 1.421413741) * t - 0.284496736) * t + 0.254829592) * t
-    rest = 0.5 * poly * tail
+    poly = ((((0.5307027145 * t - 0.7265760135) * t + 0.7107068705) * t - 0.142248368) * t + 0.127414796) * t
+    rest = poly * tail
     cdf = jnp.where(x < 0, rest, 1.0 - rest)
     return x * cdf, cdf + x * tail * 0.3989422804014327
 
@@ -574,7 +574,7 @@
     return [pltpu.SemaphoreType.DMA((count,))] * 2
 
 
-def fwd_core(group_ref, x_v, vt_v, seg, qkv, ctx, xt, lse, vec_rows, s, ticks):
+def fwd_core(group_ref, x_v, vt_v, seg, qkv, ctx, xt, lse, vec_rows, s, ticks, closing=None):
     (a_v, bias_v, oh_v, km_v, qkv_v, ka_v, va_v, ctx_v, xt_v, a_sem, out_sem) = s
     groups, length = qkv.shape[:2]
     block = 256
@@ -615,6 +615,8 @@
     xt_v[...] = flat(x_v[...]).T
     turned = pltpu.make_async_copy(xt_v, xt, a_sem.at[0])
     turned.start()
+    if closing is not None:
+        closing()
     turned.wait()
     for t in range(groups):
         pltpu.make_async_copy(qkv_v.at[t], qkv.at[t], out_sem.at[0, t]).wait()
@@ -684,8 +686,7 @@
     wait_all(rows)
     keep = copies.here(lambda: (x_v, x))
     ticks = [(1, cot_rows), (4, advance), (8, advance)]
-    fwd_core(lambda t: g.at[0, t // 2, t % 2], x_v, vt_v, seg, qkv, ctx, xt, lse, vec_rows, s, ticks)
-    advance()
+    fwd_core(lambda t: g.at[0, t // 2, t % 2], x_v, vt_v, seg, qkv, ctx, xt, lse, vec_rows, s, ticks, advance)
     for part in later:
         part.finish()
     wait_all(moved)
@@ -833,7 +834,7 @@
     )(g, x, cot, ctx, vec)
 
 
-def bwd_core(qkv, ctx, dctx, lse, seg, xt, gh1, g, da, gx, qsum, s, ticks, place=None):
+def bwd_core(qkv, ctx, dctx, lse, seg, xt, gh1, g, da, gx, qsum, s, ticks, place=None, closing=None):
     (qkv_v, ctx_v, dctx_v, a_v, oh_v, km_v, qa_v, ka_v, va_v, da_v, kt_v, dqt_v, dqkv_v, x_v, gx_v, xt_v, gt_v, dw_v, pair_v, in_sem, out_sem, x_sem, pair_sem) = s
     groups, length = qkv.shape[:2]
     block = 256
@@ -959,6 +960,8 @@
     lax.fori_loop(0, blocks, low_step, 0)
     last = pltpu.make_async_copy(x_v, gx, x_sem.at[0])
     last.start()
+    if closing is not None:
+        closing()
     for i in range(0 if place is None else early, groups):
         result(i).wait()
     last.wait()
@@ -1032,8 +1035,7 @@
         (13, functools.partial(advance, 0, 2)),
         (14, functools.partial(advance, 1, 3)),
     ]
-    bwd_core(qkv, ctx, dctx, lse, seg, xt, gh1, g, da, gx, qsum, s, ticks, place)
-    advance(0, 1, 2, 3)
+    bwd_core(qkv, ctx, dctx, lse, seg, xt, gh1, g, da, gx, qsum, s, ticks, place, functools.partial(advance, 0, 1, 2, 3))
     wait_all(moved)
 
 

time: 304 us -> 303 us (level)
  no operation moved by 1% of the time
where the time goes in v4:
time: 303 us; the launch traced here: 301 us
  Pallas kernels  285 us (94%)
  local copies, waits for them, and re-layouts  13.2 us (4%)
    pallas_call x1, Pallas kernels, fwd_comm(): pl.pallas_call(fwd_comm_kernel, in_specs=[ANY] * 4 + [VMEM], out_specs=[A...  106 us
    pallas_call x1, Pallas kernels, bwd_comm(): pl.pallas_call(bwd_comm_kernel, in_specs=[ANY] * 3 + [VMEM] * 2 + [ANY] *...  81.1 us
    pallas_call x1, Pallas kernels, middle(): pl.pallas_call(mid_kernel, in_specs=[ANY] * 4 + [VMEM], out_specs=[ANY] *...  60.6 us
    pallas_call x1, Pallas kernels, sum_comm(): pl.pallas_call(sum_comm_kernel, in_specs=[ANY] * 3, out_specs=[VMEM, VMEM...  35.2 us
    unnamed x14, local copies, waits for them, and re-layouts  6.92 us

profile of v4, /device:TPU:0, one launch (start us, length us, event | category | flops | bytes accessed | tf_op | source)
XLA Modules:
  0.0 301.5 jit_solution(3736353342573887857)
XLA Ops:
  0.7 0.7 copy-done
  1.4 0.8 copy.20
  2.1 0.6 pad.4.vec
  2.7 0.9 copy.19
  3.7 0.9 slice_bitcast_fusion.2
  4.7 0.1 concatenate.18
  4.8 1.8 pad_maximum_fusion.shard
  6.6 1.0 copy.21.seg
  7.6 105.5 %attention_forward.1 = (bf16[3,2,2,2,2,2,96,768]{7,6,5,4,3,2,1,0:T(8,128)(2,1)}, bf16[4,256,768]{2,1,0:T(8,128)(2,1)}, bf16[4,256,768]{2,1,0:T(8,128)(2,1)}, bf1...) custom-call(bf16[3,96,768]{2,1,0:T(8,128)(2,1)} %pad_maximum_fusion., ...), custom_call_target="tpu_custom_call" | custom-call | tf_op jit(solution)/shard_map/attention_forward/pallas_call | solution.py:700
  113.1 60.6 %feed_forward.1 = (bf16[4,256,768]{2,1,0:T(8,128)(2,1)}, bf16[2,4,768,768]{3,2,1,0:T(8,128)(2,1)}, f32[4,256,768]{2,1,0:T(8,128)}, bf16[4,1024,384]{2,1,0:T(8,128)(2,1)}, f32[12,8,768]{2,1,0:T(8,128)}) custom-call(bf16[3,4,768,768]{3,2,1,0:T(8,128)(2,1)} %bitcast.35, bf16[4,256,768]{2,1,0:T(8,128)(2,1)} %get-tuple-element.31.x, ...), custom_call_target="tpu_custom_call" | custom-call | tf_op jit(solution)/shard_map/feed_forward/pallas_call | solution.py:802
  173.7 81.1 %attention_backward.1 = (bf16[2,768,768]{2,1,0:T(8,128)(2,1)}, bf16[4,256,768]{2,1,0:T(8,128)(2,1)}, f32[4,8,768]{2,1,0:T(8,128)}, f32[2,96,768]{2,1,0:T(8,128)}, bf16[4,256,768]{2,1,0:T(8,128)(2,1)}) custom-call(bf16[4,1024,768]{2,1,0:T(8,128)(2,1)} %get-tuple-element.28.qkv, bf16[4,1024,384]{2,1,0:T(8,128)(2,1)} %get-tuple-element.29.ctx, ...), custom_call_target="tpu_custom_call" | custom-call | tf_op jit(solution)/shard_map/attention_backward/pallas_call | solution.py:1046
  254.8 2.4 vector_table.1
  257.2 35.2 %weight_sums.1 = (f32[96,768]{1,0:T(8,128)}, f32[24,128]{1,0:T(8,128)}, bf16[4,256,768]{2,1,0:T(8,128)(2,1)}) custom-call(bf16[2,2,2,2,96,768]{5,4,3,2,1,0:T(8,128)(2,1)} %bitcast.38, f32[2,2,2,2,2,24,128]{6,5,4,3,2,1,0:T(8,128)} %bitcast.39, bf16[4,256,768]{2,1,0:T(8,128)(2,1)} %get-tuple-element.44.gx), custom_call_target="tpu_custom_call" | custom-call | tf_op jit(solution)/shard_map/weight_sums/pallas_call | solution.py:1132
  292.4 0.8 slice_bitcast_fusion.5
  293.2 0.7 copy.24
  293.9 0.9 fusion.1
  294.8 1.1 fusion
  295.9 0.1 maximum_bitcast_fusion.3
  296.0 0.7 copy.23
  296.8 0.7 pad_maximum_fusion.1
  297.5 0.8 slice_bitcast_fusion
  298.4 1.1 copy.27
  299.5 0.8 copy-done.2
  300.4 1.1 copy.28
  (16 shorter events, 0.2 us)
Async XLA Ops:
  0.6 0.7 copy-start
  292.4 5.1 %copy-start.3 = (f32[2,96,768]{2,1,0:T(8,128)S(1)}, f32[2,96,768]{2,1,0:T(8,128)}, u32[]{:S(2)}) copy-start(f32[2,96,768]{2,1,0:T(8,128)} %get-tuple-element.47) | copy-start | bytes 1769476
  294.7 3.6 %copy-start.1 = (bf16[4,256,768]{2,1,0:T(8,128)(2,1)S(1)}, bf16[4,256,768]{2,1,0:T(8,128)(2,1)}, u32[]{:S(2)}) copy-start(bf16[4,256,768]{2,1,0:T(8,128)(2,1)} %get-tuple-element.89) | copy-start | bytes 4718596
  298.4 2.0 copy-start.2
